TPU v7x, 32 devices: a whole 2x2x4 slice. The times are simulated.
32 devices in a mesh: grp: 2 (over y), slab: 2 (over x), lat: 8 (over z, core).
Axes of the slice: x: 2, y: 2, z: 4, core: 2. Of those that a mesh axis runs over, the one named last changes fastest.
Arguments:
- cond_lists: int32 [64, 16], P(('slab', 'lat')), may hold values from 0 to 31, all different within a row
- regress: float32 [64, 128, 2048], P(('slab', 'lat')), may hold values from -0.09375 to 0.09375
- chol: float32 [64, 128, 128], P(('slab', 'lat')), as said below
- noise: float32 [128, 256, 128], P(('grp', 'slab', 'lat')), parts along dimension 0, may hold values from -6 to 6
- start_field: float32 [64, 256, 128], P(('grp', 'lat')), parts along dimension 0, may hold values from -6 to 6
Outputs:
- field: float32 [128, 256, 128], P(('grp', 'slab', 'lat')), parts along dimension 0
There are 2 independent parts, one for each index of `grp`. A program takes and returns all parts, laid end to end along the dimension named above; an argument that names none is the same for every part. Nothing has to cross between parts.
Inputs may be any that keep to these rules, and one draw needn't show every extreme that they name: `cond_lists`: each row names 16 distinct positions of the previous slab. `chol`: each factor is lower triangular with diagonal entries from 0.3 to 0.7.
All inputs are finite; a program needn't handle non-finite values.
Results may differ from a plain program's by a relative error of at most 0.0001.
Values sent between devices are 32-bit elements; how exact they have to be, the bound alone decides.
No kernel may reach another device: no remote copies, remote signals or barrier semaphores. Data moves between devices by JAX's collectives and lax.ppermute only.
A program may use at most 64 MiB of HBM per device.

v0:
```python
import jax
import jax.numpy as jnp
from jax import lax
from jax.experimental import pallas as pl
from jax.experimental.pallas import tpu as pltpu
from jax.sharding import PartitionSpec as P


def general(cond_lists, regress, chol, noise, start_field):
    blocks, _, block_size = noise.shape
    list_length = cond_lists.shape[1]
    n_slab = lax.axis_size("slab")
    slab_pos = lax.axis_index("slab")
    factors = regress.reshape(blocks, block_size, list_length, block_size)
    shock = jnp.einsum("jab,jwb->jwa", chol, noise, precision=lax.Precision.HIGHEST)

    def step(at, carry):
        source, out = carry
        previous = lax.all_gather(source, "lat", axis=0, tiled=True)
        mean = jnp.einsum("jakb,jkwb->jwa", factors, previous[cond_lists], precision=lax.Precision.HIGHEST)
        fresh = mean + shock
        out = jnp.where(at == slab_pos, fresh, out)
        source = lax.ppermute(fresh, "slab", [(i, i + 1) for i in range(n_slab - 1)])
        return source, out

    return lax.fori_loop(0, n_slab, step, (start_field, jnp.zeros_like(noise)))[1]


IN_VMEM = pl.BlockSpec(memory_space=pltpu.VMEM)
IN_HBM = pl.BlockSpec(memory_space=pltpu.HBM)
IN_SMEM = pl.BlockSpec(memory_space=pltpu.SMEM)
PARAMS = pltpu.CompilerParams(vmem_limit_bytes=12 * 2**20)


def in_hbm(x):
    return pltpu.with_memory_space_constraint(x, pltpu.HBM)


def two_parts(x):
    high = x.astype(jnp.bfloat16)
    return high, (x - high.astype(jnp.float32)).astype(jnp.bfloat16)


def products(piece_parts, slot, part_refs, blocks, size):
    high, _, both = piece_parts
    front = high.shape[0]
    first = slot * blocks
    out = []
    high_ref, low_ref = part_refs
    columns = high_ref.shape[2]
    step = min(columns, 2 * size)
    for at in range(0, columns, step):
        w_high = high_ref[first:first + blocks, :, at:at + step].reshape(blocks * size, step)
        w_low = low_ref[first:first + blocks, :, at:at + step].reshape(blocks * size, step)
        product = jnp.dot(both, w_high, preferred_element_type=jnp.float32)
        product = product[:front] + product[front:] + jnp.dot(high, w_low, preferred_element_type=jnp.float32)
        out += [product[:, i:i + size] for i in range(0, step, size)]
    return out


def piece_parts(piece):
    high, low = two_parts(piece)
    return high, low, jnp.concatenate([high, low], axis=0)


def added(base, pieces, slots, parts):
    blocks, _, size = base.shape

    def kernel(base_ref, *refs):
        n = len(pieces)
        out_ref = refs[-1]
        total = None
        for i in range(n):
            piece = piece_parts(jnp.concatenate([refs[i][p] for p in range(blocks)], axis=1))
            terms = products(piece, slots[i], refs[n:n + 2], blocks, size)
            total = terms if total is None else [t + u for t, u in zip(total, terms)]
        for i in range(blocks):
            out_ref[i] = base_ref[i] + total[i]

    return pl.pallas_call(
        kernel,
        out_shape=jax.ShapeDtypeStruct(base.shape, jnp.float32),
        in_specs=[IN_VMEM] * (len(pieces) + 3),
        out_specs=IN_VMEM,
        compiler_params=PARAMS,
    )(base, *pieces, *parts)


def placed(turned_from, at, count, size, rows_ref, high_ref, low_ref):
    def one(k, carry):
        row = rows_ref[at * count + k]
        high, low = two_parts(turned_from(pl.ds(pl.multiple_of(k * size, size), size)).T)
        high_ref[row, :, at * size:(at + 1) * size] = high
        low_ref[row, :, at * size:(at + 1) * size] = low
        return carry

    lax.fori_loop(0, count, one, 0, unroll=4 if count % 4 == 0 else 1)


def weights(rows, regress, places):
    blocks, size, width = regress.shape
    count = width // size

    def kernel(rows_ref, regress_ref, high_ref, low_ref, buffer, arrived):
        def fetch(at):
            return pltpu.make_async_copy(regress_ref.at[at], buffer.at[at % 2], arrived.at[at % 2])

        fetch(0).start()
        high_ref[...] = jnp.zeros_like(high_ref)
        low_ref[...] = jnp.zeros_like(low_ref)
        for at in range(blocks):
            fetch(at).wait()
            if at + 1 < blocks:
                fetch(at + 1).start()
            placed(lambda ks, at=at: buffer[at % 2, :, ks], at, count, size, rows_ref, high_ref, low_ref)

    part = pltpu.VMEM((places, size, 2 * blocks * size), jnp.bfloat16)
    return pl.pallas_call(
        kernel,
        out_shape=(part,) * 2,
        in_specs=[IN_SMEM, IN_HBM],
        out_specs=(IN_VMEM,) * 2,
        scratch_shapes=[pltpu.VMEM((2, size, width), jnp.float32), pltpu.SemaphoreType.DMA((2,))],
        compiler_params=PARAMS,
        name="weights",
    )(rows, in_hbm(regress))


def weights_other(rows, parts, regress_other):
    blocks, size, width = regress_other.shape
    count = width // size

    def kernel(rows_ref, high_in, low_in, regress_ref, high_ref, low_ref):
        del high_in, low_in
        for at in range(blocks):
            placed(lambda ks, at=at: regress_ref[at, :, ks], blocks + at, count, size, rows_ref, high_ref, low_ref)

    part = pltpu.VMEM(parts[0].shape, jnp.bfloat16)
    return pl.pallas_call(
        kernel,
        out_shape=(part,) * 2,
        in_specs=[IN_SMEM] + [IN_VMEM] * 3,
        out_specs=(IN_VMEM,) * 2,
        input_output_aliases={1: 0, 2: 1},
        compiler_params=PARAMS,
        name="weights_other",
    )(rows, *parts, regress_other)


def opening(core_at, parts, chol, noise, start, chol_other, noise_other, start_other):
    blocks, nreal, size = noise.shape
    half = nreal // 2
    quarter = half // 2

    def kernel(core_ref, high_ref, low_ref, chol_hbm, noise_hbm, start_hbm, chol_o_ref, noise_o_ref, start_o_ref, *refs):
        outs, (chol_ref, noise_ref, start_ref, arrived) = refs[:4], refs[4:]
        here = pl.multiple_of(core_ref[0] * half, half)
        copies = [
            pltpu.make_async_copy(chol_hbm, chol_ref, arrived.at[0]),
            pltpu.make_async_copy(noise_hbm.at[:, pl.ds(here, half), :], noise_ref, arrived.at[1]),
            pltpu.make_async_copy(start_hbm.at[:, pl.ds(here, half), :], start_ref, arrived.at[2]),
        ]
        for copy in copies:
            copy.start()
        for copy in copies:
            copy.wait()
        own = [start_ref[i] for i in range(blocks)] + [start_o_ref[i, pl.ds(here, half), :] for i in range(blocks)]
        terms = products(piece_parts(jnp.concatenate(own, axis=1)), 0, (high_ref, low_ref), 2 * blocks, size)
        for at in range(2 * blocks):
            i = at % blocks
            high, _, both = piece_parts(noise_ref[i] if at < blocks else noise_o_ref[i, pl.ds(here, half), :])
            c_high, c_low = two_parts((chol_ref if at < blocks else chol_o_ref)[i].T)
            shock = jnp.dot(both, c_high, preferred_element_type=jnp.float32)
            shock = shock[:half] + shock[half:] + jnp.dot(high, c_low, preferred_element_type=jnp.float32)
            for q in (0, 1):
                outs[q][at] = shock[q * quarter:(q + 1) * quarter]
                outs[2 + q][at] = shock[q * quarter:(q + 1) * quarter] + terms[at][q * quarter:(q + 1) * quarter]

    piece = jax.ShapeDtypeStruct((2 * blocks, quarter, size), jnp.float32)
    held = pltpu.VMEM((blocks, half, size), jnp.float32)
    return pl.pallas_call(
        kernel,
        out_shape=(piece,) * 4,
        in_specs=[IN_SMEM] + [IN_VMEM] * 2 + [IN_HBM] * 3 + [IN_VMEM] * 3,
        out_specs=(IN_VMEM,) * 4,
        scratch_shapes=[pltpu.VMEM(chol.shape, jnp.float32), held, held, pltpu.SemaphoreType.DMA((3,))],
        compiler_params=PARAMS,
        name="opening",
    )(core_at, *parts, in_hbm(chol), in_hbm(noise), in_hbm(start), chol_other, noise_other, start_other)


def paired(cond_lists, regress, chol, noise, start_field):
    blocks, nreal, _ = noise.shape
    half, quarter = nreal // 2, nreal // 4
    slab = lax.axis_index("slab")
    lat = lax.axis_index("lat")
    place, core = lax.div(lat, 2), lax.rem(lat, 2)

    def along_lat(pairs):
        both = [(a, b) for a, b in pairs] + [(b, a) for a, b in pairs]
        wires = [(2 * a + c, 2 * b + c) for a, b in both for c in (0, 1)]
        return lambda x: lax.ppermute(x, "lat", wires)

    even, odd, far = along_lat([(0, 1), (2, 3)]), along_lat([(1, 2)]), along_lat([(0, 3), (1, 2)])

    def across(x):
        return lax.ppermute(x, "slab", [(0, 1), (1, 0)])

    def partner(x):
        return lax.ppermute(x, "lat", [(i, i ^ 1) for i in range(8)])

    start_other = partner(start_field)
    lists_other = partner(cond_lists)

    def rows_of(lists):
        there = lax.div(lists, 2 * blocks)
        inside = lax.rem(lists, 2 * blocks)
        return ((there ^ place) * (2 * blocks) + (lax.div(inside, blocks) ^ core) * blocks + lax.rem(inside, blocks)).reshape(-1)

    rows = jnp.concatenate([rows_of(cond_lists), rows_of(lists_other)])
    scalars = (slab == 0, (place == 0) | (place == 3), core == 0, core.reshape(1), core * half + slab * quarter, rows)
    scalars, start_other, regress, chol, noise = lax.optimization_barrier((scalars, start_other, regress, chol, noise))
    on_first, at_end, core_first, core_at, first, rows = scalars
    chol_other = partner(chol)
    noise_other = partner(noise)
    regress_other = partner(regress)

    mine = jnp.concatenate([lax.dynamic_slice_in_dim(x, first, quarter, 1) for x in (start_field, start_other)], 0)
    d1 = far(mine)
    e1 = even(mine)
    d1_x = across(d1)
    e2 = even(d1)
    o2 = odd(e1)
    e1_x = across(e1)
    s1 = jnp.where(at_end, e2, o2)
    parts = weights(rows, regress, 8 * blocks)
    parts = weights_other(rows, parts, regress_other)
    shock_1, shock_2, base_1, base_2 = opening(
        core_at, parts, chol, noise, start_field, chol_other, noise_other, start_other)
    direct = added(base_1, [e1, d1], [1, 3], parts)
    direct = added(direct, [s1], [2], parts)
    crossed = across(jnp.where(on_first, direct, s1))
    routed = added(base_2, [e1_x, d1_x], [1, 3], parts)
    routed = added(routed, [crossed], [2], parts)

    own_x = across(routed)
    own = jnp.where(on_first, routed, crossed)
    f2 = far(own)
    f1 = even(own)
    f2_x = across(f2)
    g2 = even(f2)
    h2 = odd(f1)
    f1_x = across(f1)
    f3 = jnp.where(at_end, g2, h2)
    f3_x = across(f3)
    direct_b = added(shock_1, [crossed, f1, f2], [0, 1, 3], parts)
    direct_b = added(direct_b, [f3], [2], parts)
    routed_b = added(shock_2, [own_x, f1_x, f2_x], [0, 1, 3], parts)
    routed_b = added(routed_b, [f3_x], [2], parts)

    def home(x):
        back = partner(x[blocks:])
        return x[:blocks], back

    near_a, back_a = home(jnp.where(on_first, direct, direct_b))
    near_b, back_b = home(jnp.where(on_first, routed, routed_b))
    near = jnp.concatenate([near_a, near_b], 1)
    back = jnp.concatenate([back_a, back_b], 1)
    return jnp.where(core_first, jnp.concatenate([near, back], 1), jnp.concatenate([back, near], 1))


def solution(mesh):
    sizes = dict(mesh.shape)

    def shards(cond_lists, regress, chol, noise, start_field):
        args = (cond_lists, regress, chol, noise, start_field)
        fits = sizes["slab"] == 2 and sizes["lat"] == 8 and noise.shape[1] % 32 == 0 and noise.shape[2] % 128 == 0
        if not fits:
            return general(*args)
        return paired(*args)

    in_specs = (
        P(("slab", "lat"), None),
        P(("slab", "lat"), None, None),
        P(("slab", "lat"), None, None),
        P(("grp", "slab", "lat"), None, None),
        P(("grp", "lat"), None, None),
    )
    out_specs = P(("grp", "slab", "lat"), None, None)
    return jax.shard_map(shards, mesh=mesh, in_specs=in_specs, out_specs=out_specs, check_vma=False)
```

profile of v0, /device:TPU:0, one launch (start us, length us, event | category | flops | bytes accessed | tf_op | source)
XLA Modules:
  0.0 93.2 jit_solution(3546935172150819136)
XLA Ops:
  1.7 0.9 collective-permute-done.1.start_o_ref
  2.8 0.9 constant_dynamic-slice_fusion.1
  3.7 5.0 %collective-permute-start.6 = (f32[8,64,128]{2,1,0:T(8,128)S(1)}, f32[8,64,128]{2,1,0:T(8,128)S(1)}, u32[]{:S(2)}, u32[]{:S(2)}) collective-permute-start(f32[8,64,128]{2,1,0:T(8,128)S(1)} %pad_maximum_fusion), channel_id=1, source_target_pairs={{0,6},{1,7},{2,4},{3,5},{6,0},{7,1},{4,2},{5,3},{8,14},{9,15},{10,... | collective-permute-start | bytes 786440 | tf_op jit(solution)/shard_map/ppermute | solution.py:202
  8.8 7.2 %collective-permute-done.6.refs_1_ = f32[8,64,128]{2,1,0:T(8,128)S(1)} collective-permute-done((f32[8,64,128]{2,1,0:T(8,128)S(1)}, f32[8,64,128]{2,1,0:T(8,128)S(1)}, u32[]{:S(2)}, u32[]{:S(2)}) %collective-permute-start.6) | collective-permute-done | bytes 262176 | tf_op jit(solution)/shard_map/ppermute | solution.py:202
  16.0 4.7 %collective-permute-start.7 = (f32[8,64,128]{2,1,0:T(8,128)S(1)}, f32[8,64,128]{2,1,0:T(8,128)S(1)}, u32[]{:S(2)}, u32[]{:S(2)}) collective-permute-start(f32[8,64,128]{2,1,0:T(8,128)S(1)} %collective-permute-done.6.refs_1_), channel_id=1, source_target_pairs={{0,2},{1,3},{4,6},{5,7},{2,0},{3,1},{6,4},{7,5},{8,10},{9,11},{12,... | collective-permute-start | bytes 786440 | tf_op jit(solution)/shard_map/ppermute | solution.py:202
  21.9 6.1 %weights.1 = (bf16[32,128,1024]{2,1,0:T(8,128)(2,1)S(1)}, bf16[32,128,1024]{2,1,0:T(8,128)(2,1)S(1)}) custom-call(s32[128]{0:T(128)S(1)} %pad_add_fusion.rows_ref, f32[4,128,2048]{2,1,0:T(8,128)} %regress_ref), custom_call_target="tpu_custom_call" | custom-call | tf_op jit(solution)/shard_map/weights/pallas_call | solution.py:118
  28.1 1.6 %collective-permute-start.10 = (f32[8,64,128]{2,1,0:T(8,128)S(1)}, f32[8,64,128]{2,1,0:T(8,128)S(1)}, u32[]{:S(2)}, u32[]{:S(2)}) collective-permute-start(f32[8,64,128]{2,1,0:T(8,128)S(1)} %collective-permute-done.5.refs_0_), channel_id=1, source_target_pairs={{0,8},{8,0},{1,9},{9,1},{2,10},{10,2},{3,11},{11,3},{4,12},{12,4},... | collective-permute-start | bytes 786440 | tf_op jit(solution)/shard_map/ppermute | solution.py:207
  30.2 4.8 %weights_other.1 = (bf16[32,128,1024]{2,1,0:T(8,128)(2,1)S(1)}, bf16[32,128,1024]{2,1,0:T(8,128)(2,1)S(1)}) custom-call(s32[128]{0:T(128)S(1)} %pad_add_fusion.rows_ref, bf16[32,128,1024]{2,1,0:T(8,128)(2,1)S(1)} %get-tuple-element.28.high_in, bf16[32,128,1024]{2,1,0:T(8,128)(2,1)S(1)} %get-tuple-element.29.low_in, ...), custom_call_target="tpu_custom_call", output_to_operand_aliasing={{0}: (1, {}), {1}: (2, {})} | custom-call | tf_op jit(solution)/shard_map/weights_other/pallas_call | solution.py:139
  35.0 2.3 %opening.1 = (f32[8,64,128]{2,1,0:T(8,128)S(1)}, f32[8,64,128]{2,1,0:T(8,128)S(1)}, f32[8,64,128]{2,1,0:T(8,128)S(1)}, f32[8,64,128]{2,1,0:T(8,128)S(1)}) custom-call(s32[1]{0:T(128)} %bitcast.core_ref, bf16[32,128,1024]{2,1,0:T(8,128)(2,1)S(1)} %get-tuple-element.30.high_ref.refs_2_.refs_1_.refs_3_, ...), custom_call_target="tpu_custom_call" | custom-call | tf_op jit(solution)/shard_map/opening/pallas_call | solution.py:181
  37.4 1.5 %shard_map.60.base_ref = f32[8,64,128]{2,1,0:T(8,128)S(1)} custom-call(f32[8,64,128]{2,1,0:T(8,128)S(1)} %get-tuple-element.35.base_ref, f32[8,64,128]{2,1,0:T(8,128)S(1)} %collective-permute-done.5.refs_0_, f32[8,64,128]{2,1,0:T(8,128)S(1)} %collective-permute-done.6.refs_1_, bf16[32,128,1024]{2,1,0:T(8,128)(2,1)S(1)} %get-tuple-element.30.high_ref.refs_2_.refs_1_.refs_3_, ...), custom_call_target="tpu_custom_call" | custom-call | tf_op jit(solution)/shard_map/pallas_call | solution.py:80
  38.8 0.8 shard_map.61
  39.7 1.5 %collective-permute-start.9 = (f32[8,64,128]{2,1,0:T(8,128)S(1)}, f32[8,64,128]{2,1,0:T(8,128)S(1)}, u32[]{:S(2)}, u32[]{:S(2)}) collective-permute-start(f32[8,64,128]{2,1,0:T(8,128)S(1)} %broadcast_select_fusion.5), channel_id=1, source_target_pairs={{0,8},{8,0},{1,9},{9,1},{2,10},{10,2},{3,11},{11,3},{4,12},{12,4},... | collective-permute-start | bytes 786440 | tf_op jit(solution)/shard_map/ppermute | solution.py:207
  41.2 1.4 %collective-permute-done.11.refs_1_ = f32[8,64,128]{2,1,0:T(8,128)S(1)} collective-permute-done((f32[8,64,128]{2,1,0:T(8,128)S(1)}, f32[8,64,128]{2,1,0:T(8,128)S(1)}, u32[]{:S(2)}, u32[]{:S(2)}) %collective-permute-start.11) | collective-permute-done | bytes 262176 | tf_op jit(solution)/shard_map/ppermute | solution.py:207
  42.6 1.5 %shard_map.62.base_ref = f32[8,64,128]{2,1,0:T(8,128)S(1)} custom-call(f32[8,64,128]{2,1,0:T(8,128)S(1)} %get-tuple-element.39.base_ref, f32[8,64,128]{2,1,0:T(8,128)S(1)} %collective-permute-done.10.refs_0_, f32[8,64,128]{2,1,0:T(8,128)S(1)} %collective-permute-done.11.refs_1_, ...), custom_call_target="tpu_custom_call" | custom-call | tf_op jit(solution)/shard_map/pallas_call | solution.py:80
  44.1 4.0 %collective-permute-done.9.refs_0_ = f32[8,64,128]{2,1,0:T(8,128)S(1)} collective-permute-done((f32[8,64,128]{2,1,0:T(8,128)S(1)}, f32[8,64,128]{2,1,0:T(8,128)S(1)}, u32[]{:S(2)}, u32[]{:S(2)}) %collective-permute-start.9) | collective-permute-done | bytes 262176 | tf_op jit(solution)/shard_map/ppermute | solution.py:207
  48.9 2.1 %collective-permute-start.13 = (f32[8,64,128]{2,1,0:T(8,128)S(1)}, f32[8,64,128]{2,1,0:T(8,128)S(1)}, u32[]{:S(2)}, u32[]{:S(2)}) collective-permute-start(f32[8,64,128]{2,1,0:T(8,128)S(1)} %broadcast_select_fusion.4), channel_id=1, source_target_pairs={{0,6},{1,7},{2,4},{3,5},{6,0},{7,1},{4,2},{5,3},{8,14},{9,15},{10,... | collective-permute-start | bytes 786440 | tf_op jit(solution)/shard_map/ppermute | solution.py:202
  51.0 3.0 %collective-permute-start.12 = (f32[8,64,128]{2,1,0:T(8,128)S(1)}, f32[8,64,128]{2,1,0:T(8,128)S(1)}, u32[]{:S(2)}, u32[]{:S(2)}) collective-permute-start(f32[8,64,128]{2,1,0:T(8,128)S(1)} %broadcast_select_fusion.4), channel_id=1, source_target_pairs={{0,2},{1,3},{4,6},{5,7},{2,0},{3,1},{6,4},{7,5},{8,10},{9,11},{12,... | collective-permute-start | bytes 786440 | tf_op jit(solution)/shard_map/ppermute | solution.py:202
  54.0 6.0 %collective-permute-done.13.refs_2_ = f32[8,64,128]{2,1,0:T(8,128)S(1)} collective-permute-done((f32[8,64,128]{2,1,0:T(8,128)S(1)}, f32[8,64,128]{2,1,0:T(8,128)S(1)}, u32[]{:S(2)}, u32[]{:S(2)}) %collective-permute-start.13) | collective-permute-done | bytes 262176 | tf_op jit(solution)/shard_map/ppermute | solution.py:202
  60.0 4.4 %collective-permute-start.14 = (f32[8,64,128]{2,1,0:T(8,128)S(1)}, f32[8,64,128]{2,1,0:T(8,128)S(1)}, u32[]{:S(2)}, u32[]{:S(2)}) collective-permute-start(f32[8,64,128]{2,1,0:T(8,128)S(1)} %collective-permute-done.13.refs_2_), channel_id=1, source_target_pairs={{0,2},{1,3},{4,6},{5,7},{2,0},{3,1},{6,4},{7,5},{8,10},{9,11},{12,... | collective-permute-start | bytes 786440 | tf_op jit(solution)/shard_map/ppermute | solution.py:202
  64.4 0.8 collective-permute-start.15
  65.3 1.6 %collective-permute-start.16 = (f32[8,64,128]{2,1,0:T(8,128)S(1)}, f32[8,64,128]{2,1,0:T(8,128)S(1)}, u32[]{:S(2)}, u32[]{:S(2)}) collective-permute-start(f32[8,64,128]{2,1,0:T(8,128)S(1)} %shard_map.63), channel_id=1, source_target_pairs={{0,8},{8,0},{1,9},{9,1},{2,10},{10,2},{3,11},{11,3},{4,12},{12,4},... | collective-permute-start | bytes 786440 | tf_op jit(solution)/shard_map/ppermute | solution.py:207
  67.4 1.5 %collective-permute-start.18 = (f32[8,64,128]{2,1,0:T(8,128)S(1)}, f32[8,64,128]{2,1,0:T(8,128)S(1)}, u32[]{:S(2)}, u32[]{:S(2)}) collective-permute-start(f32[8,64,128]{2,1,0:T(8,128)S(1)} %collective-permute-done.13.refs_2_), channel_id=1, source_target_pairs={{0,8},{8,0},{1,9},{9,1},{2,10},{10,2},{3,11},{11,3},{4,12},{12,4},... | collective-permute-start | bytes 786440 | tf_op jit(solution)/shard_map/ppermute | solution.py:207
  68.9 2.1 %shard_map.64.base_ref = f32[8,64,128]{2,1,0:T(8,128)S(1)} custom-call(f32[8,64,128]{2,1,0:T(8,128)S(1)} %get-tuple-element.38.base_ref, f32[8,64,128]{2,1,0:T(8,128)S(1)} %collective-permute-done.9.refs_0_, f32[8,64,128]{2,1,0:T(8,128)S(1)} %collective-permute-done.12.refs_1_, f32[8,64,128]{2,1,0:T(8,128)S(1)} %collective-permute-done.13.refs_2_, ...), custom_call_target="tpu_custom_call" | custom-call | tf_op jit(solution)/shard_map/pallas_call | solution.py:80
  71.1 1.4 %collective-permute-start.19 = (f32[8,64,128]{2,1,0:T(8,128)S(1)}, f32[8,64,128]{2,1,0:T(8,128)S(1)}, u32[]{:S(2)}, u32[]{:S(2)}) collective-permute-start(f32[8,64,128]{2,1,0:T(8,128)S(1)} %broadcast_select_fusion.refs_0_), channel_id=1, source_target_pairs={{0,8},{8,0},{1,9},{9,1},{2,10},{10,2},{3,11},{11,3},{4,12},{12,4},... | collective-permute-start | bytes 786440 | tf_op jit(solution)/shard_map/ppermute | solution.py:207
  72.5 0.8 shard_map.65
  73.4 1.1 %collective-permute-done.16.refs_0_ = f32[8,64,128]{2,1,0:T(8,128)S(1)} collective-permute-done((f32[8,64,128]{2,1,0:T(8,128)S(1)}, f32[8,64,128]{2,1,0:T(8,128)S(1)}, u32[]{:S(2)}, u32[]{:S(2)}) %collective-permute-start.16) | collective-permute-done | bytes 262176 | tf_op jit(solution)/shard_map/ppermute | solution.py:207
  74.5 5.6 %collective-permute-done.17.refs_1_ = f32[8,64,128]{2,1,0:T(8,128)S(1)} collective-permute-done((f32[8,64,128]{2,1,0:T(8,128)S(1)}, f32[8,64,128]{2,1,0:T(8,128)S(1)}, u32[]{:S(2)}, u32[]{:S(2)}) %collective-permute-start.17) | collective-permute-done | bytes 262176 | tf_op jit(solution)/shard_map/ppermute | solution.py:207
  80.1 5.6 %collective-permute-done.18.refs_2_ = f32[8,64,128]{2,1,0:T(8,128)S(1)} collective-permute-done((f32[8,64,128]{2,1,0:T(8,128)S(1)}, f32[8,64,128]{2,1,0:T(8,128)S(1)}, u32[]{:S(2)}, u32[]{:S(2)}) %collective-permute-start.18) | collective-permute-done | bytes 262176 | tf_op jit(solution)/shard_map/ppermute | solution.py:207
  85.7 2.1 %shard_map.66.base_ref = f32[8,64,128]{2,1,0:T(8,128)S(1)} custom-call(f32[8,64,128]{2,1,0:T(8,128)S(1)} %get-tuple-element.40.base_ref, f32[8,64,128]{2,1,0:T(8,128)S(1)} %collective-permute-done.16.refs_0_, f32[8,64,128]{2,1,0:T(8,128)S(1)} %collective-permute-done.17.refs_1_, f32[8,64,128]{2,1,0:T(8,128)S(1)} %collective-permute-done.18.refs_2_, ...), custom_call_target="tpu_custom_call" | custom-call | tf_op jit(solution)/shard_map/pallas_call | solution.py:80
  87.9 2.2 %collective-permute-done.19.refs_0_ = f32[8,64,128]{2,1,0:T(8,128)S(1)} collective-permute-done((f32[8,64,128]{2,1,0:T(8,128)S(1)}, f32[8,64,128]{2,1,0:T(8,128)S(1)}, u32[]{:S(2)}, u32[]{:S(2)}) %collective-permute-start.19) | collective-permute-done | bytes 262176 | tf_op jit(solution)/shard_map/ppermute | solution.py:207
  91.1 1.3 %collective-permute-done.21 = f32[4,64,128]{2,1,0:T(8,128)S(1)} collective-permute-done((f32[4,64,128]{2,1,0:T(8,128)S(1)}, f32[4,64,128]{2,1,0:T(8,128)S(1)}, u32[]{:S(2)}, u32[]{:S(2)}) %collective-permute-start.21) | collective-permute-done | bytes 131104 | tf_op jit(solution)/shard_map/ppermute | solution.py:210
  92.4 0.8 maximum_select_fusion
  (40 shorter events, 6.1 us)
Async XLA Ops:
  0.0 1.5 %collective-permute-start = (s32[4,16]{1,0:T(4,128)}, s32[4,16]{1,0:T(4,128)S(1)}, u32[]{:S(2)}, u32[]{:S(2)}) collective-permute-start(s32[4,16]{1,0:T(4,128)} %param.5), channel_id=1, source_target_pairs={{0,1},{1,0},{2,3},{3,2},{4,5},{5,4},{6,7},{7,6},{8,9},{9,8},{10,11... | collective-permute-start | bytes 776 | tf_op jit(solution)/shard_map/ppermute | solution.py:210
  0.5 2.1 %collective-permute-start.1 = (f32[4,256,128]{2,1,0:T(8,128)}, f32[4,256,128]{2,1,0:T(8,128)S(1)}, u32[]{:S(2)}, u32[]{:S(2)}) collective-permute-start(f32[4,256,128]{2,1,0:T(8,128)} %start_hbm.1), channel_id=1, source_target_pairs={{0,1},{1,0},{2,3},{3,2},{4,5},{5,4},{6,7},{7,6},{8,9},{9,8},{10,11... | collective-permute-start | bytes 1572872 | tf_op jit(solution)/shard_map/ppermute | solution.py:210
  2.6 27.6 %collective-permute-start.2 = (f32[4,128,2048]{2,1,0:T(8,128)}, f32[4,128,2048]{2,1,0:T(8,128)}, u32[]{:S(2)}, u32[]{:S(2)}) collective-permute-start(f32[4,128,2048]{2,1,0:T(8,128)} %regress_ref), channel_id=1, source_target_pairs={{0,1},{1,0},{2,3},{3,2},{4,5},{5,4},{6,7},{7,6},{8,9},{9,8},{10,11... | collective-permute-start | bytes 12582920 | tf_op jit(solution)/shard_map/ppermute | solution.py:210
  3.7 12.3 %collective-permute-start.6 = (f32[8,64,128]{2,1,0:T(8,128)S(1)}, f32[8,64,128]{2,1,0:T(8,128)S(1)}, u32[]{:S(2)}, u32[]{:S(2)}) collective-permute-start(f32[8,64,128]{2,1,0:T(8,128)S(1)} %pad_maximum_fusion), channel_id=1, source_target_pairs={{0,6},{1,7},{2,4},{3,5},{6,0},{7,1},{4,2},{5,3},{8,14},{9,15},{10,... | collective-permute-start | bytes 786440 | tf_op jit(solution)/shard_map/ppermute | solution.py:202
  8.8 12.4 %collective-permute-start.5 = (f32[8,64,128]{2,1,0:T(8,128)S(1)}, f32[8,64,128]{2,1,0:T(8,128)S(1)}, u32[]{:S(2)}, u32[]{:S(2)}) collective-permute-start(f32[8,64,128]{2,1,0:T(8,128)S(1)} %pad_maximum_fusion), channel_id=1, source_target_pairs={{0,2},{1,3},{4,6},{5,7},{2,0},{3,1},{6,4},{7,5},{8,10},{9,11},{12,... | collective-permute-start | bytes 786440 | tf_op jit(solution)/shard_map/ppermute | solution.py:202
  8.8 26.2 %collective-permute-start.4 = (f32[4,256,128]{2,1,0:T(8,128)}, f32[4,256,128]{2,1,0:T(8,128)S(1)}, u32[]{:S(2)}, u32[]{:S(2)}) collective-permute-start(f32[4,256,128]{2,1,0:T(8,128)} %noise_hbm), channel_id=1, source_target_pairs={{0,1},{1,0},{2,3},{3,2},{4,5},{5,4},{6,7},{7,6},{8,9},{9,8},{10,11... | collective-permute-start | bytes 1572872 | tf_op jit(solution)/shard_map/ppermute | solution.py:210
  16.0 12.0 %collective-permute-start.7 = (f32[8,64,128]{2,1,0:T(8,128)S(1)}, f32[8,64,128]{2,1,0:T(8,128)S(1)}, u32[]{:S(2)}, u32[]{:S(2)}) collective-permute-start(f32[8,64,128]{2,1,0:T(8,128)S(1)} %collective-permute-done.6.refs_1_), channel_id=1, source_target_pairs={{0,2},{1,3},{4,6},{5,7},{2,0},{3,1},{6,4},{7,5},{8,10},{9,11},{12,... | collective-permute-start | bytes 786440 | tf_op jit(solution)/shard_map/ppermute | solution.py:202
  21.2 8.4 %collective-permute-start.8 = (f32[8,64,128]{2,1,0:T(8,128)S(1)}, f32[8,64,128]{2,1,0:T(8,128)S(1)}, u32[]{:S(2)}, u32[]{:S(2)}) collective-permute-start(f32[8,64,128]{2,1,0:T(8,128)S(1)} %collective-permute-done.5.refs_0_), channel_id=1, source_target_pairs={{2,4},{3,5},{4,2},{5,3},{10,12},{11,13},{12,10},{13,11},{18,20},{1... | collective-permute-start | bytes 786440 | tf_op jit(solution)/shard_map/ppermute | solution.py:202
  21.9 13.1 %collective-permute-start.3 = (f32[4,128,128]{2,1,0:T(8,128)}, f32[4,128,128]{2,1,0:T(8,128)S(1)}, u32[]{:S(2)}, u32[]{:S(2)}) collective-permute-start(f32[4,128,128]{2,1,0:T(8,128)} %chol_hbm), channel_id=1, source_target_pairs={{0,1},{1,0},{2,3},{3,2},{4,5},{5,4},{6,7},{7,6},{8,9},{9,8},{10,11... | collective-permute-start | bytes 786440 | tf_op jit(solution)/shard_map/ppermute | solution.py:210
  28.1 13.2 %collective-permute-start.10 = (f32[8,64,128]{2,1,0:T(8,128)S(1)}, f32[8,64,128]{2,1,0:T(8,128)S(1)}, u32[]{:S(2)}, u32[]{:S(2)}) collective-permute-start(f32[8,64,128]{2,1,0:T(8,128)S(1)} %collective-permute-done.5.refs_0_), channel_id=1, source_target_pairs={{0,8},{8,0},{1,9},{9,1},{2,10},{10,2},{3,11},{11,3},{4,12},{12,4},... | collective-permute-start | bytes 786440 | tf_op jit(solution)/shard_map/ppermute | solution.py:207
  29.6 13.0 %collective-permute-start.11 = (f32[8,64,128]{2,1,0:T(8,128)S(1)}, f32[8,64,128]{2,1,0:T(8,128)S(1)}, u32[]{:S(2)}, u32[]{:S(2)}) collective-permute-start(f32[8,64,128]{2,1,0:T(8,128)S(1)} %collective-permute-done.6.refs_1_), channel_id=1, source_target_pairs={{0,8},{8,0},{1,9},{9,1},{2,10},{10,2},{3,11},{11,3},{4,12},{12,4},... | collective-permute-start | bytes 786440 | tf_op jit(solution)/shard_map/ppermute | solution.py:207
  39.7 8.4 %collective-permute-start.9 = (f32[8,64,128]{2,1,0:T(8,128)S(1)}, f32[8,64,128]{2,1,0:T(8,128)S(1)}, u32[]{:S(2)}, u32[]{:S(2)}) collective-permute-start(f32[8,64,128]{2,1,0:T(8,128)S(1)} %broadcast_select_fusion.5), channel_id=1, source_target_pairs={{0,8},{8,0},{1,9},{9,1},{2,10},{10,2},{3,11},{11,3},{4,12},{12,4},... | collective-permute-start | bytes 786440 | tf_op jit(solution)/shard_map/ppermute | solution.py:207
  48.9 11.1 %collective-permute-start.13 = (f32[8,64,128]{2,1,0:T(8,128)S(1)}, f32[8,64,128]{2,1,0:T(8,128)S(1)}, u32[]{:S(2)}, u32[]{:S(2)}) collective-permute-start(f32[8,64,128]{2,1,0:T(8,128)S(1)} %broadcast_select_fusion.4), channel_id=1, source_target_pairs={{0,6},{1,7},{2,4},{3,5},{6,0},{7,1},{4,2},{5,3},{8,14},{9,15},{10,... | collective-permute-start | bytes 786440 | tf_op jit(solution)/shard_map/ppermute | solution.py:202
  51.0 13.4 %collective-permute-start.12 = (f32[8,64,128]{2,1,0:T(8,128)S(1)}, f32[8,64,128]{2,1,0:T(8,128)S(1)}, u32[]{:S(2)}, u32[]{:S(2)}) collective-permute-start(f32[8,64,128]{2,1,0:T(8,128)S(1)} %broadcast_select_fusion.4), channel_id=1, source_target_pairs={{0,2},{1,3},{4,6},{5,7},{2,0},{3,1},{6,4},{7,5},{8,10},{9,11},{12,... | collective-permute-start | bytes 786440 | tf_op jit(solution)/shard_map/ppermute | solution.py:202
  60.0 11.0 %collective-permute-start.14 = (f32[8,64,128]{2,1,0:T(8,128)S(1)}, f32[8,64,128]{2,1,0:T(8,128)S(1)}, u32[]{:S(2)}, u32[]{:S(2)}) collective-permute-start(f32[8,64,128]{2,1,0:T(8,128)S(1)} %collective-permute-done.13.refs_2_), channel_id=1, source_target_pairs={{0,2},{1,3},{4,6},{5,7},{2,0},{3,1},{6,4},{7,5},{8,10},{9,11},{12,... | collective-permute-start | bytes 786440 | tf_op jit(solution)/shard_map/ppermute | solution.py:202
  64.4 6.6 %collective-permute-start.15 = (f32[8,64,128]{2,1,0:T(8,128)S(1)}, f32[8,64,128]{2,1,0:T(8,128)S(1)}, u32[]{:S(2)}, u32[]{:S(2)}) collective-permute-start(f32[8,64,128]{2,1,0:T(8,128)S(1)} %collective-permute-done.12.refs_1_), channel_id=1, source_target_pairs={{2,4},{3,5},{4,2},{5,3},{10,12},{11,13},{12,10},{13,11},{18,20},{1... | collective-permute-start | bytes 786440 | tf_op jit(solution)/shard_map/ppermute | solution.py:202
  65.3 9.2 %collective-permute-start.16 = (f32[8,64,128]{2,1,0:T(8,128)S(1)}, f32[8,64,128]{2,1,0:T(8,128)S(1)}, u32[]{:S(2)}, u32[]{:S(2)}) collective-permute-start(f32[8,64,128]{2,1,0:T(8,128)S(1)} %shard_map.63), channel_id=1, source_target_pairs={{0,8},{8,0},{1,9},{9,1},{2,10},{10,2},{3,11},{11,3},{4,12},{12,4},... | collective-permute-start | bytes 786440 | tf_op jit(solution)/shard_map/ppermute | solution.py:207
  66.8 13.3 %collective-permute-start.17 = (f32[8,64,128]{2,1,0:T(8,128)S(1)}, f32[8,64,128]{2,1,0:T(8,128)S(1)}, u32[]{:S(2)}, u32[]{:S(2)}) collective-permute-start(f32[8,64,128]{2,1,0:T(8,128)S(1)} %collective-permute-done.12.refs_1_), channel_id=1, source_target_pairs={{0,8},{8,0},{1,9},{9,1},{2,10},{10,2},{3,11},{11,3},{4,12},{12,4},... | collective-permute-start | bytes 786440 | tf_op jit(solution)/shard_map/ppermute | solution.py:207
  67.4 18.4 %collective-permute-start.18 = (f32[8,64,128]{2,1,0:T(8,128)S(1)}, f32[8,64,128]{2,1,0:T(8,128)S(1)}, u32[]{:S(2)}, u32[]{:S(2)}) collective-permute-start(f32[8,64,128]{2,1,0:T(8,128)S(1)} %collective-permute-done.13.refs_2_), channel_id=1, source_target_pairs={{0,8},{8,0},{1,9},{9,1},{2,10},{10,2},{3,11},{11,3},{4,12},{12,4},... | collective-permute-start | bytes 786440 | tf_op jit(solution)/shard_map/ppermute | solution.py:207
  71.1 19.1 %collective-permute-start.19 = (f32[8,64,128]{2,1,0:T(8,128)S(1)}, f32[8,64,128]{2,1,0:T(8,128)S(1)}, u32[]{:S(2)}, u32[]{:S(2)}) collective-permute-start(f32[8,64,128]{2,1,0:T(8,128)S(1)} %broadcast_select_fusion.refs_0_), channel_id=1, source_target_pairs={{0,8},{8,0},{1,9},{9,1},{2,10},{10,2},{3,11},{11,3},{4,12},{12,4},... | collective-permute-start | bytes 786440 | tf_op jit(solution)/shard_map/ppermute | solution.py:207
  73.4 17.7 %collective-permute-start.20 = (f32[4,64,128]{2,1,0:T(8,128)S(1)}, f32[4,64,128]{2,1,0:T(8,128)S(1)}, u32[]{:S(2)}, u32[]{:S(2)}) collective-permute-start(f32[4,64,128]{2,1,0:T(8,128)S(1)} %get-tuple-element.42), channel_id=1, source_target_pairs={{0,1},{1,0},{2,3},{3,2},{4,5},{5,4},{6,7},{7,6},{8,9},{9,8},{10,11... | collective-permute-start | bytes 393224 | tf_op jit(solution)/shard_map/ppermute | solution.py:210
  91.0 1.4 %collective-permute-start.21 = (f32[4,64,128]{2,1,0:T(8,128)S(1)}, f32[4,64,128]{2,1,0:T(8,128)S(1)}, u32[]{:S(2)}, u32[]{:S(2)}) collective-permute-start(f32[4,64,128]{2,1,0:T(8,128)S(1)} %get-tuple-element.44), channel_id=1, source_target_pairs={{0,1},{1,0},{2,3},{3,2},{4,5},{5,4},{6,7},{7,6},{8,9},{9,8},{10,11... | collective-permute-start | bytes 393224 | tf_op jit(solution)/shard_map/ppermute | solution.py:210
where the time goes:
time: 93.6 us; the launch traced here: 93.2 us
  waiting for transfers between devices  36.1 us (39%)
  starting transfers between devices  30.3 us (32%)
  Pallas kernels  23.6 us (25%)
  other arithmetic  1.83 us (2%)
  local copies, waits for them, and re-layouts  1.16 us (1%)
    ppermute x8, starting transfers between devices, along_lat(): return lambda x: lax.ppermute(x, 'lat', wires)  20.8 us
    ppermute x7, waiting for transfers between devices, across(): return lax.ppermute(x, 'slab', [(0, 1), (1, 0)])  19.9 us
    ppermute x8, waiting for transfers between devices, along_lat(): return lambda x: lax.ppermute(x, 'lat', wires)  13.7 us
    pallas_call x8, Pallas kernels, added(): pl.pallas_call(kernel, out_shape=jax.ShapeDtypeStruct(base.shape, jnp.flo...  10.4 us
    ppermute x7, starting transfers between devices, across(): return lax.ppermute(x, 'slab', [(0, 1), (1, 0)])  8.65 us
    pallas_call x1, Pallas kernels, weights(): pl.pallas_call(kernel, out_shape=(part,) * 2, in_specs=[IN_SMEM, IN_HBM],...  6.1 us
    pallas_call x1, Pallas kernels, weights_other(): pl.pallas_call(kernel, out_shape=(part,) * 2, in_specs=[IN_SMEM] + [IN_VM...  4.79 us
    ppermute x7, waiting for transfers between devices, partner(): return lax.ppermute(x, 'lat', [(i, i ^ 1) for i in range(8)])  2.48 us
  transfers between devices with their start and end apart: 22, of which 12 were waited for; matrix products, arithmetic and copies ran while one was open for 2% of the time, Pallas kernels for 25%

commit v1 on v0

--- a/solution.py
+++ b/solution.py
@@ -94,7 +94,7 @@
         low_ref[row, :, at * size:(at + 1) * size] = low
         return carry
 
-    lax.fori_loop(0, count, one, 0, unroll=4 if count % 4 == 0 else 1)
+    lax.fori_loop(0, count, one, 0, unroll=True)
 
 
 def weights(rows, regress, places):
@@ -102,17 +102,14 @@
     count = width // size
 
     def kernel(rows_ref, regress_ref, high_ref, low_ref, buffer, arrived):
-        def fetch(at):
-            return pltpu.make_async_copy(regress_ref.at[at], buffer.at[at % 2], arrived.at[at % 2])
-
-        fetch(0).start()
+        copies = [pltpu.make_async_copy(regress_ref.at[at], buffer.at[at], arrived.at[at]) for at in range(blocks)]
+        for copy in copies:
+            copy.start()
         high_ref[...] = jnp.zeros_like(high_ref)
         low_ref[...] = jnp.zeros_like(low_ref)
         for at in range(blocks):
-            fetch(at).wait()
-            if at + 1 < blocks:
-                fetch(at + 1).start()
-            placed(lambda ks, at=at: buffer[at % 2, :, ks], at, count, size, rows_ref, high_ref, low_ref)
+            copies[at].wait()
+            placed(lambda ks, at=at: buffer[at, :, ks], at, count, size, rows_ref, high_ref, low_ref)
 
     part = pltpu.VMEM((places, size, 2 * blocks * size), jnp.bfloat16)
     return pl.pallas_call(
@@ -120,7 +117,7 @@
         out_shape=(part,) * 2,
         in_specs=[IN_SMEM, IN_HBM],
         out_specs=(IN_VMEM,) * 2,
-        scratch_shapes=[pltpu.VMEM((2, size, width), jnp.float32), pltpu.SemaphoreType.DMA((2,))],
+        scratch_shapes=[pltpu.VMEM(regress.shape, jnp.float32), pltpu.SemaphoreType.DMA((blocks,))],
         compiler_params=PARAMS,
         name="weights",
     )(rows, in_hbm(regress))
@@ -210,6 +207,7 @@
         return lax.ppermute(x, "lat", [(i, i ^ 1) for i in range(8)])
 
     start_other = partner(start_field)
+    mine = lax.dynamic_slice_in_dim(start_field, core * half + slab * quarter, quarter, 1)
     lists_other = partner(cond_lists)
 
     def rows_of(lists):
@@ -218,14 +216,14 @@
         return ((there ^ place) * (2 * blocks) + (lax.div(inside, blocks) ^ core) * blocks + lax.rem(inside, blocks)).reshape(-1)
 
     rows = jnp.concatenate([rows_of(cond_lists), rows_of(lists_other)])
-    scalars = (slab == 0, (place == 0) | (place == 3), core == 0, core.reshape(1), core * half + slab * quarter, rows)
+    scalars = (slab == 0, (place == 0) | (place == 3), core == 0, core.reshape(1), core * half + slab * quarter, rows, mine)
     scalars, start_other, regress, chol, noise = lax.optimization_barrier((scalars, start_other, regress, chol, noise))
-    on_first, at_end, core_first, core_at, first, rows = scalars
+    on_first, at_end, core_first, core_at, first, rows, mine = scalars
     chol_other = partner(chol)
     noise_other = partner(noise)
     regress_other = partner(regress)
 
-    mine = jnp.concatenate([lax.dynamic_slice_in_dim(x, first, quarter, 1) for x in (start_field, start_other)], 0)
+    mine = jnp.concatenate([mine, lax.dynamic_slice_in_dim(start_other, first, quarter, 1)], 0)
     d1 = far(mine)
     e1 = even(mine)
     d1_x = across(d1)

time: 93.6 us -> 89.7 us (0.958)
  Pallas kernels: 23.6 us -> 19.9 us
    pallas_call x1, Pallas kernels: 6.1 us -> 3.53 us  [weights(): pl.pallas_call(kernel, out_shape=(part,) * 2, in_specs=[IN_SMEM, IN_HBM],...]
    ppermute x8, waiting for transfers between devices: 13.7 us -> 15.1 us  [along_lat(): return lambda x: lax.ppermute(x, 'lat', wires)]
    pallas_call x1, Pallas kernels: 4.79 us -> 3.69 us  [weights_other(): pl.pallas_call(kernel, out_shape=(part,) * 2, in_specs=[IN_SMEM] + [IN_VM...]
  transfers between devices with their start and end apart: 22 -> 22, of which waited for: 12 -> 12; matrix products, arithmetic and copies ran while one was open for 2% -> 2% of each run, Pallas kernels for 25% -> 21%
where the time goes in v1:
time: 89.7 us; the launch traced here: 89.5 us
  waiting for transfers between devices  36.5 us (41%)
  starting transfers between devices  29.8 us (33%)
  Pallas kernels  19.9 us (22%)
  other arithmetic  1.83 us (2%)
  local copies, waits for them, and re-layouts  1.14 us (1%)
    ppermute x8, starting transfers between devices, along_lat(): return lambda x: lax.ppermute(x, 'lat', wires)  20.2 us
    ppermute x7, waiting for transfers between devices, across(): return lax.ppermute(x, 'slab', [(0, 1), (1, 0)])  19.8 us
    ppermute x8, waiting for transfers between devices, along_lat(): return lambda x: lax.ppermute(x, 'lat', wires)  15.1 us
    pallas_call x8, Pallas kernels, added(): pl.pallas_call(kernel, out_shape=jax.ShapeDtypeStruct(base.shape, jnp.flo...  10.4 us
    ppermute x7, starting transfers between devices, across(): return lax.ppermute(x, 'slab', [(0, 1), (1, 0)])  8.58 us
    pallas_call x1, Pallas kernels, weights_other(): pl.pallas_call(kernel, out_shape=(part,) * 2, in_specs=[IN_SMEM] + [IN_VM...  3.69 us
    pallas_call x1, Pallas kernels, weights(): pl.pallas_call(kernel, out_shape=(part,) * 2, in_specs=[IN_SMEM, IN_HBM],...  3.53 us
    pallas_call x1, Pallas kernels, opening(): pl.pallas_call(kernel, out_shape=(piece,) * 4, in_specs=[IN_SMEM] + [IN_V...  2.33 us
  transfers between devices with their start and end apart: 22, of which 12 were waited for; matrix products, arithmetic and copies ran while one was open for 2% of the time, Pallas kernels for 21%

profile of v1, /device:TPU:0, one launch (start us, length us, event | category | flops | bytes accessed | tf_op | source)
XLA Modules:
  0.0 89.5 jit_solution(5813507360114803011)
XLA Ops:
  0.5 0.9 %constant_dynamic-slice_fusion.1 = f32[4,64,128]{2,1,0:T(8,128)S(1)} fusion(f32[4,256,128]{2,1,0:T(8,128)} %start_hbm.1, s32[]{:T(128)S(6)} %select_n.44), kind=kLoop, calls=%fused_computation.34 | loop fusion | bytes 262148 | tf_op jit(solution)/shard_map/dynamic_slice | solution.py:210
  2.9 4.9 %collective-permute-start.6 = (f32[8,64,128]{2,1,0:T(8,128)S(1)}, f32[8,64,128]{2,1,0:T(8,128)S(1)}, u32[]{:S(2)}, u32[]{:S(2)}) collective-permute-start(f32[8,64,128]{2,1,0:T(8,128)S(1)} %pad_maximum_fusion), channel_id=1, source_target_pairs={{0,6},{1,7},{2,4},{3,5},{6,0},{7,1},{4,2},{5,3},{8,14},{9,15},{10,... | collective-permute-start | bytes 786440 | tf_op jit(solution)/shard_map/ppermute | solution.py:199
  7.8 7.2 %collective-permute-done.6.refs_1_ = f32[8,64,128]{2,1,0:T(8,128)S(1)} collective-permute-done((f32[8,64,128]{2,1,0:T(8,128)S(1)}, f32[8,64,128]{2,1,0:T(8,128)S(1)}, u32[]{:S(2)}, u32[]{:S(2)}) %collective-permute-start.6) | collective-permute-done | bytes 262176 | tf_op jit(solution)/shard_map/ppermute | solution.py:199
  15.1 4.8 %collective-permute-start.7 = (f32[8,64,128]{2,1,0:T(8,128)S(1)}, f32[8,64,128]{2,1,0:T(8,128)S(1)}, u32[]{:S(2)}, u32[]{:S(2)}) collective-permute-start(f32[8,64,128]{2,1,0:T(8,128)S(1)} %collective-permute-done.6.refs_1_), channel_id=1, source_target_pairs={{0,2},{1,3},{4,6},{5,7},{2,0},{3,1},{6,4},{7,5},{8,10},{9,11},{12,... | collective-permute-start | bytes 786440 | tf_op jit(solution)/shard_map/ppermute | solution.py:199
  21.1 3.5 %weights.1 = (bf16[32,128,1024]{2,1,0:T(8,128)(2,1)S(1)}, bf16[32,128,1024]{2,1,0:T(8,128)(2,1)S(1)}) custom-call(s32[128]{0:T(128)S(1)} %pad_add_fusion.rows_ref, f32[4,128,2048]{2,1,0:T(8,128)} %regress_ref), custom_call_target="tpu_custom_call" | custom-call | tf_op jit(solution)/shard_map/weights/pallas_call | solution.py:115
  24.7 1.2 %collective-permute-done.7 = f32[8,64,128]{2,1,0:T(8,128)S(1)} collective-permute-done((f32[8,64,128]{2,1,0:T(8,128)S(1)}, f32[8,64,128]{2,1,0:T(8,128)S(1)}, u32[]{:S(2)}, u32[]{:S(2)}) %collective-permute-start.7) | collective-permute-done | bytes 262176 | tf_op jit(solution)/shard_map/ppermute | solution.py:199
  25.9 1.5 %collective-permute-start.10 = (f32[8,64,128]{2,1,0:T(8,128)S(1)}, f32[8,64,128]{2,1,0:T(8,128)S(1)}, u32[]{:S(2)}, u32[]{:S(2)}) collective-permute-start(f32[8,64,128]{2,1,0:T(8,128)S(1)} %collective-permute-done.5.refs_0_), channel_id=1, source_target_pairs={{0,8},{8,0},{1,9},{9,1},{2,10},{10,2},{3,11},{11,3},{4,12},{12,4},... | collective-permute-start | bytes 786440 | tf_op jit(solution)/shard_map/ppermute | solution.py:204
  28.0 3.7 %weights_other.1 = (bf16[32,128,1024]{2,1,0:T(8,128)(2,1)S(1)}, bf16[32,128,1024]{2,1,0:T(8,128)(2,1)S(1)}) custom-call(s32[128]{0:T(128)S(1)} %pad_add_fusion.rows_ref, bf16[32,128,1024]{2,1,0:T(8,128)(2,1)S(1)} %get-tuple-element.29.high_in, bf16[32,128,1024]{2,1,0:T(8,128)(2,1)S(1)} %get-tuple-element.30.low_in, ...), custom_call_target="tpu_custom_call", output_to_operand_aliasing={{0}: (1, {}), {1}: (2, {})} | custom-call | tf_op jit(solution)/shard_map/weights_other/pallas_call | solution.py:136
  31.7 2.3 %opening.1 = (f32[8,64,128]{2,1,0:T(8,128)S(1)}, f32[8,64,128]{2,1,0:T(8,128)S(1)}, f32[8,64,128]{2,1,0:T(8,128)S(1)}, f32[8,64,128]{2,1,0:T(8,128)S(1)}) custom-call(s32[1]{0:T(128)} %bitcast.core_ref, bf16[32,128,1024]{2,1,0:T(8,128)(2,1)S(1)} %get-tuple-element.31.high_ref.refs_2_.refs_1_.refs_3_, ...), custom_call_target="tpu_custom_call" | custom-call | tf_op jit(solution)/shard_map/opening/pallas_call | solution.py:178
  34.0 1.5 %shard_map.60.base_ref = f32[8,64,128]{2,1,0:T(8,128)S(1)} custom-call(f32[8,64,128]{2,1,0:T(8,128)S(1)} %get-tuple-element.36.base_ref, f32[8,64,128]{2,1,0:T(8,128)S(1)} %collective-permute-done.5.refs_0_, f32[8,64,128]{2,1,0:T(8,128)S(1)} %collective-permute-done.6.refs_1_, bf16[32,128,1024]{2,1,0:T(8,128)(2,1)S(1)} %get-tuple-element.31.high_ref.refs_2_.refs_1_.refs_3_, ...), custom_call_target="tpu_custom_call" | custom-call | tf_op jit(solution)/shard_map/pallas_call | solution.py:80
  35.5 0.8 shard_map.61
  36.4 1.6 %collective-permute-start.9 = (f32[8,64,128]{2,1,0:T(8,128)S(1)}, f32[8,64,128]{2,1,0:T(8,128)S(1)}, u32[]{:S(2)}, u32[]{:S(2)}) collective-permute-start(f32[8,64,128]{2,1,0:T(8,128)S(1)} %broadcast_select_fusion.5), channel_id=1, source_target_pairs={{0,8},{8,0},{1,9},{9,1},{2,10},{10,2},{3,11},{11,3},{4,12},{12,4},... | collective-permute-start | bytes 786440 | tf_op jit(solution)/shard_map/ppermute | solution.py:204
  37.9 2.4 %collective-permute-done.11.refs_1_ = f32[8,64,128]{2,1,0:T(8,128)S(1)} collective-permute-done((f32[8,64,128]{2,1,0:T(8,128)S(1)}, f32[8,64,128]{2,1,0:T(8,128)S(1)}, u32[]{:S(2)}, u32[]{:S(2)}) %collective-permute-start.11) | collective-permute-done | bytes 262176 | tf_op jit(solution)/shard_map/ppermute | solution.py:204
  40.4 1.5 %shard_map.62.base_ref = f32[8,64,128]{2,1,0:T(8,128)S(1)} custom-call(f32[8,64,128]{2,1,0:T(8,128)S(1)} %get-tuple-element.41.base_ref, f32[8,64,128]{2,1,0:T(8,128)S(1)} %collective-permute-done.10.refs_0_, f32[8,64,128]{2,1,0:T(8,128)S(1)} %collective-permute-done.11.refs_1_, ...), custom_call_target="tpu_custom_call" | custom-call | tf_op jit(solution)/shard_map/pallas_call | solution.py:80
  41.8 2.9 %collective-permute-done.9.refs_0_ = f32[8,64,128]{2,1,0:T(8,128)S(1)} collective-permute-done((f32[8,64,128]{2,1,0:T(8,128)S(1)}, f32[8,64,128]{2,1,0:T(8,128)S(1)}, u32[]{:S(2)}, u32[]{:S(2)}) %collective-permute-start.9) | collective-permute-done | bytes 262176 | tf_op jit(solution)/shard_map/ppermute | solution.py:204
  45.5 2.1 %collective-permute-start.13 = (f32[8,64,128]{2,1,0:T(8,128)S(1)}, f32[8,64,128]{2,1,0:T(8,128)S(1)}, u32[]{:S(2)}, u32[]{:S(2)}) collective-permute-start(f32[8,64,128]{2,1,0:T(8,128)S(1)} %broadcast_select_fusion.4), channel_id=1, source_target_pairs={{0,6},{1,7},{2,4},{3,5},{6,0},{7,1},{4,2},{5,3},{8,14},{9,15},{10,... | collective-permute-start | bytes 786440 | tf_op jit(solution)/shard_map/ppermute | solution.py:199
  47.6 2.9 %collective-permute-start.12 = (f32[8,64,128]{2,1,0:T(8,128)S(1)}, f32[8,64,128]{2,1,0:T(8,128)S(1)}, u32[]{:S(2)}, u32[]{:S(2)}) collective-permute-start(f32[8,64,128]{2,1,0:T(8,128)S(1)} %broadcast_select_fusion.4), channel_id=1, source_target_pairs={{0,2},{1,3},{4,6},{5,7},{2,0},{3,1},{6,4},{7,5},{8,10},{9,11},{12,... | collective-permute-start | bytes 786440 | tf_op jit(solution)/shard_map/ppermute | solution.py:199
  50.5 6.1 %collective-permute-done.13.refs_2_ = f32[8,64,128]{2,1,0:T(8,128)S(1)} collective-permute-done((f32[8,64,128]{2,1,0:T(8,128)S(1)}, f32[8,64,128]{2,1,0:T(8,128)S(1)}, u32[]{:S(2)}, u32[]{:S(2)}) %collective-permute-start.13) | collective-permute-done | bytes 262176 | tf_op jit(solution)/shard_map/ppermute | solution.py:199
  56.6 4.0 %collective-permute-start.14 = (f32[8,64,128]{2,1,0:T(8,128)S(1)}, f32[8,64,128]{2,1,0:T(8,128)S(1)}, u32[]{:S(2)}, u32[]{:S(2)}) collective-permute-start(f32[8,64,128]{2,1,0:T(8,128)S(1)} %collective-permute-done.13.refs_2_), channel_id=1, source_target_pairs={{0,2},{1,3},{4,6},{5,7},{2,0},{3,1},{6,4},{7,5},{8,10},{9,11},{12,... | collective-permute-start | bytes 786440 | tf_op jit(solution)/shard_map/ppermute | solution.py:199
  60.6 0.8 collective-permute-start.15
  61.5 1.6 %collective-permute-start.16 = (f32[8,64,128]{2,1,0:T(8,128)S(1)}, f32[8,64,128]{2,1,0:T(8,128)S(1)}, u32[]{:S(2)}, u32[]{:S(2)}) collective-permute-start(f32[8,64,128]{2,1,0:T(8,128)S(1)} %shard_map.63), channel_id=1, source_target_pairs={{0,8},{8,0},{1,9},{9,1},{2,10},{10,2},{3,11},{11,3},{4,12},{12,4},... | collective-permute-start | bytes 786440 | tf_op jit(solution)/shard_map/ppermute | solution.py:204
  63.6 1.5 %collective-permute-start.18 = (f32[8,64,128]{2,1,0:T(8,128)S(1)}, f32[8,64,128]{2,1,0:T(8,128)S(1)}, u32[]{:S(2)}, u32[]{:S(2)}) collective-permute-start(f32[8,64,128]{2,1,0:T(8,128)S(1)} %collective-permute-done.13.refs_2_), channel_id=1, source_target_pairs={{0,8},{8,0},{1,9},{9,1},{2,10},{10,2},{3,11},{11,3},{4,12},{12,4},... | collective-permute-start | bytes 786440 | tf_op jit(solution)/shard_map/ppermute | solution.py:204
  65.0 2.1 %shard_map.64.base_ref = f32[8,64,128]{2,1,0:T(8,128)S(1)} custom-call(f32[8,64,128]{2,1,0:T(8,128)S(1)} %get-tuple-element.40.base_ref, f32[8,64,128]{2,1,0:T(8,128)S(1)} %collective-permute-done.9.refs_0_, f32[8,64,128]{2,1,0:T(8,128)S(1)} %collective-permute-done.12.refs_1_, f32[8,64,128]{2,1,0:T(8,128)S(1)} %collective-permute-done.13.refs_2_, ...), custom_call_target="tpu_custom_call" | custom-call | tf_op jit(solution)/shard_map/pallas_call | solution.py:80
  67.3 1.4 %collective-permute-start.19 = (f32[8,64,128]{2,1,0:T(8,128)S(1)}, f32[8,64,128]{2,1,0:T(8,128)S(1)}, u32[]{:S(2)}, u32[]{:S(2)}) collective-permute-start(f32[8,64,128]{2,1,0:T(8,128)S(1)} %broadcast_select_fusion.refs_0_), channel_id=1, source_target_pairs={{0,8},{8,0},{1,9},{9,1},{2,10},{10,2},{3,11},{11,3},{4,12},{12,4},... | collective-permute-start | bytes 786440 | tf_op jit(solution)/shard_map/ppermute | solution.py:204
  69.6 1.1 %collective-permute-done.16.refs_0_ = f32[8,64,128]{2,1,0:T(8,128)S(1)} collective-permute-done((f32[8,64,128]{2,1,0:T(8,128)S(1)}, f32[8,64,128]{2,1,0:T(8,128)S(1)}, u32[]{:S(2)}, u32[]{:S(2)}) %collective-permute-start.16) | collective-permute-done | bytes 262176 | tf_op jit(solution)/shard_map/ppermute | solution.py:204
  70.7 5.6 %collective-permute-done.17.refs_1_ = f32[8,64,128]{2,1,0:T(8,128)S(1)} collective-permute-done((f32[8,64,128]{2,1,0:T(8,128)S(1)}, f32[8,64,128]{2,1,0:T(8,128)S(1)}, u32[]{:S(2)}, u32[]{:S(2)}) %collective-permute-start.17) | collective-permute-done | bytes 262176 | tf_op jit(solution)/shard_map/ppermute | solution.py:204
  76.3 5.6 %collective-permute-done.18.refs_2_ = f32[8,64,128]{2,1,0:T(8,128)S(1)} collective-permute-done((f32[8,64,128]{2,1,0:T(8,128)S(1)}, f32[8,64,128]{2,1,0:T(8,128)S(1)}, u32[]{:S(2)}, u32[]{:S(2)}) %collective-permute-start.18) | collective-permute-done | bytes 262176 | tf_op jit(solution)/shard_map/ppermute | solution.py:204
  81.9 2.1 %shard_map.66.base_ref = f32[8,64,128]{2,1,0:T(8,128)S(1)} custom-call(f32[8,64,128]{2,1,0:T(8,128)S(1)} %get-tuple-element.42.base_ref, f32[8,64,128]{2,1,0:T(8,128)S(1)} %collective-permute-done.16.refs_0_, f32[8,64,128]{2,1,0:T(8,128)S(1)} %collective-permute-done.17.refs_1_, f32[8,64,128]{2,1,0:T(8,128)S(1)} %collective-permute-done.18.refs_2_, ...), custom_call_target="tpu_custom_call" | custom-call | tf_op jit(solution)/shard_map/pallas_call | solution.py:80
  84.1 2.2 %collective-permute-done.19.refs_0_ = f32[8,64,128]{2,1,0:T(8,128)S(1)} collective-permute-done((f32[8,64,128]{2,1,0:T(8,128)S(1)}, f32[8,64,128]{2,1,0:T(8,128)S(1)}, u32[]{:S(2)}, u32[]{:S(2)}) %collective-permute-start.19) | collective-permute-done | bytes 262176 | tf_op jit(solution)/shard_map/ppermute | solution.py:204
  86.3 0.8 shard_map.67
  87.3 1.3 %collective-permute-done.21 = f32[4,64,128]{2,1,0:T(8,128)S(1)} collective-permute-done((f32[4,64,128]{2,1,0:T(8,128)S(1)}, f32[4,64,128]{2,1,0:T(8,128)S(1)}, u32[]{:S(2)}, u32[]{:S(2)}) %collective-permute-start.21) | collective-permute-done | bytes 131104 | tf_op jit(solution)/shard_map/ppermute | solution.py:207
  88.6 0.8 maximum_select_fusion
  (40 shorter events, 6.3 us)
Async XLA Ops:
  0.0 2.2 %collective-permute-start = (s32[4,16]{1,0:T(4,128)}, s32[4,16]{1,0:T(4,128)S(1)}, u32[]{:S(2)}, u32[]{:S(2)}) collective-permute-start(s32[4,16]{1,0:T(4,128)} %param.5), channel_id=1, source_target_pairs={{0,1},{1,0},{2,3},{3,2},{4,5},{5,4},{6,7},{7,6},{8,9},{9,8},{10,11... | collective-permute-start | bytes 776 | tf_op jit(solution)/shard_map/ppermute | solution.py:207
  0.5 2.1 %collective-permute-start.1 = (f32[4,256,128]{2,1,0:T(8,128)}, f32[4,256,128]{2,1,0:T(8,128)S(1)}, u32[]{:S(2)}, u32[]{:S(2)}) collective-permute-start(f32[4,256,128]{2,1,0:T(8,128)} %start_hbm.1), channel_id=1, source_target_pairs={{0,1},{1,0},{2,3},{3,2},{4,5},{5,4},{6,7},{7,6},{8,9},{9,8},{10,11... | collective-permute-start | bytes 1572872 | tf_op jit(solution)/shard_map/ppermute | solution.py:207
  2.6 25.4 %collective-permute-start.2 = (f32[4,128,2048]{2,1,0:T(8,128)}, f32[4,128,2048]{2,1,0:T(8,128)}, u32[]{:S(2)}, u32[]{:S(2)}) collective-permute-start(f32[4,128,2048]{2,1,0:T(8,128)} %regress_ref), channel_id=1, source_target_pairs={{0,1},{1,0},{2,3},{3,2},{4,5},{5,4},{6,7},{7,6},{8,9},{9,8},{10,11... | collective-permute-start | bytes 12582920 | tf_op jit(solution)/shard_map/ppermute | solution.py:207
  2.9 12.1 %collective-permute-start.6 = (f32[8,64,128]{2,1,0:T(8,128)S(1)}, f32[8,64,128]{2,1,0:T(8,128)S(1)}, u32[]{:S(2)}, u32[]{:S(2)}) collective-permute-start(f32[8,64,128]{2,1,0:T(8,128)S(1)} %pad_maximum_fusion), channel_id=1, source_target_pairs={{0,6},{1,7},{2,4},{3,5},{6,0},{7,1},{4,2},{5,3},{8,14},{9,15},{10,... | collective-permute-start | bytes 786440 | tf_op jit(solution)/shard_map/ppermute | solution.py:199
  7.8 12.6 %collective-permute-start.5 = (f32[8,64,128]{2,1,0:T(8,128)S(1)}, f32[8,64,128]{2,1,0:T(8,128)S(1)}, u32[]{:S(2)}, u32[]{:S(2)}) collective-permute-start(f32[8,64,128]{2,1,0:T(8,128)S(1)} %pad_maximum_fusion), channel_id=1, source_target_pairs={{0,2},{1,3},{4,6},{5,7},{2,0},{3,1},{6,4},{7,5},{8,10},{9,11},{12,... | collective-permute-start | bytes 786440 | tf_op jit(solution)/shard_map/ppermute | solution.py:199
  7.8 23.9 %collective-permute-start.4 = (f32[4,256,128]{2,1,0:T(8,128)}, f32[4,256,128]{2,1,0:T(8,128)S(1)}, u32[]{:S(2)}, u32[]{:S(2)}) collective-permute-start(f32[4,256,128]{2,1,0:T(8,128)} %noise_hbm), channel_id=1, source_target_pairs={{0,1},{1,0},{2,3},{3,2},{4,5},{5,4},{6,7},{7,6},{8,9},{9,8},{10,11... | collective-permute-start | bytes 1572872 | tf_op jit(solution)/shard_map/ppermute | solution.py:207
  15.1 10.8 %collective-permute-start.7 = (f32[8,64,128]{2,1,0:T(8,128)S(1)}, f32[8,64,128]{2,1,0:T(8,128)S(1)}, u32[]{:S(2)}, u32[]{:S(2)}) collective-permute-start(f32[8,64,128]{2,1,0:T(8,128)S(1)} %collective-permute-done.6.refs_1_), channel_id=1, source_target_pairs={{0,2},{1,3},{4,6},{5,7},{2,0},{3,1},{6,4},{7,5},{8,10},{9,11},{12,... | collective-permute-start | bytes 786440 | tf_op jit(solution)/shard_map/ppermute | solution.py:199
  20.4 7.0 %collective-permute-start.8 = (f32[8,64,128]{2,1,0:T(8,128)S(1)}, f32[8,64,128]{2,1,0:T(8,128)S(1)}, u32[]{:S(2)}, u32[]{:S(2)}) collective-permute-start(f32[8,64,128]{2,1,0:T(8,128)S(1)} %collective-permute-done.5.refs_0_), channel_id=1, source_target_pairs={{2,4},{3,5},{4,2},{5,3},{10,12},{11,13},{12,10},{13,11},{18,20},{1... | collective-permute-start | bytes 786440 | tf_op jit(solution)/shard_map/ppermute | solution.py:199
  21.1 10.6 %collective-permute-start.3 = (f32[4,128,128]{2,1,0:T(8,128)}, f32[4,128,128]{2,1,0:T(8,128)S(1)}, u32[]{:S(2)}, u32[]{:S(2)}) collective-permute-start(f32[4,128,128]{2,1,0:T(8,128)} %chol_hbm), channel_id=1, source_target_pairs={{0,1},{1,0},{2,3},{3,2},{4,5},{5,4},{6,7},{7,6},{8,9},{9,8},{10,11... | collective-permute-start | bytes 786440 | tf_op jit(solution)/shard_map/ppermute | solution.py:207
  25.9 12.0 %collective-permute-start.10 = (f32[8,64,128]{2,1,0:T(8,128)S(1)}, f32[8,64,128]{2,1,0:T(8,128)S(1)}, u32[]{:S(2)}, u32[]{:S(2)}) collective-permute-start(f32[8,64,128]{2,1,0:T(8,128)S(1)} %collective-permute-done.5.refs_0_), channel_id=1, source_target_pairs={{0,8},{8,0},{1,9},{9,1},{2,10},{10,2},{3,11},{11,3},{4,12},{12,4},... | collective-permute-start | bytes 786440 | tf_op jit(solution)/shard_map/ppermute | solution.py:204
  27.4 12.9 %collective-permute-start.11 = (f32[8,64,128]{2,1,0:T(8,128)S(1)}, f32[8,64,128]{2,1,0:T(8,128)S(1)}, u32[]{:S(2)}, u32[]{:S(2)}) collective-permute-start(f32[8,64,128]{2,1,0:T(8,128)S(1)} %collective-permute-done.6.refs_1_), channel_id=1, source_target_pairs={{0,8},{8,0},{1,9},{9,1},{2,10},{10,2},{3,11},{11,3},{4,12},{12,4},... | collective-permute-start | bytes 786440 | tf_op jit(solution)/shard_map/ppermute | solution.py:204
  36.4 8.3 %collective-permute-start.9 = (f32[8,64,128]{2,1,0:T(8,128)S(1)}, f32[8,64,128]{2,1,0:T(8,128)S(1)}, u32[]{:S(2)}, u32[]{:S(2)}) collective-permute-start(f32[8,64,128]{2,1,0:T(8,128)S(1)} %broadcast_select_fusion.5), channel_id=1, source_target_pairs={{0,8},{8,0},{1,9},{9,1},{2,10},{10,2},{3,11},{11,3},{4,12},{12,4},... | collective-permute-start | bytes 786440 | tf_op jit(solution)/shard_map/ppermute | solution.py:204
  45.5 11.1 %collective-permute-start.13 = (f32[8,64,128]{2,1,0:T(8,128)S(1)}, f32[8,64,128]{2,1,0:T(8,128)S(1)}, u32[]{:S(2)}, u32[]{:S(2)}) collective-permute-start(f32[8,64,128]{2,1,0:T(8,128)S(1)} %broadcast_select_fusion.4), channel_id=1, source_target_pairs={{0,6},{1,7},{2,4},{3,5},{6,0},{7,1},{4,2},{5,3},{8,14},{9,15},{10,... | collective-permute-start | bytes 786440 | tf_op jit(solution)/shard_map/ppermute | solution.py:199
  47.6 13.0 %collective-permute-start.12 = (f32[8,64,128]{2,1,0:T(8,128)S(1)}, f32[8,64,128]{2,1,0:T(8,128)S(1)}, u32[]{:S(2)}, u32[]{:S(2)}) collective-permute-start(f32[8,64,128]{2,1,0:T(8,128)S(1)} %broadcast_select_fusion.4), channel_id=1, source_target_pairs={{0,2},{1,3},{4,6},{5,7},{2,0},{3,1},{6,4},{7,5},{8,10},{9,11},{12,... | collective-permute-start | bytes 786440 | tf_op jit(solution)/shard_map/ppermute | solution.py:199
  56.6 10.6 %collective-permute-start.14 = (f32[8,64,128]{2,1,0:T(8,128)S(1)}, f32[8,64,128]{2,1,0:T(8,128)S(1)}, u32[]{:S(2)}, u32[]{:S(2)}) collective-permute-start(f32[8,64,128]{2,1,0:T(8,128)S(1)} %collective-permute-done.13.refs_2_), channel_id=1, source_target_pairs={{0,2},{1,3},{4,6},{5,7},{2,0},{3,1},{6,4},{7,5},{8,10},{9,11},{12,... | collective-permute-start | bytes 786440 | tf_op jit(solution)/shard_map/ppermute | solution.py:199
  60.6 6.6 %collective-permute-start.15 = (f32[8,64,128]{2,1,0:T(8,128)S(1)}, f32[8,64,128]{2,1,0:T(8,128)S(1)}, u32[]{:S(2)}, u32[]{:S(2)}) collective-permute-start(f32[8,64,128]{2,1,0:T(8,128)S(1)} %collective-permute-done.12.refs_1_), channel_id=1, source_target_pairs={{2,4},{3,5},{4,2},{5,3},{10,12},{11,13},{12,10},{13,11},{18,20},{1... | collective-permute-start | bytes 786440 | tf_op jit(solution)/shard_map/ppermute | solution.py:199
  61.5 9.2 %collective-permute-start.16 = (f32[8,64,128]{2,1,0:T(8,128)S(1)}, f32[8,64,128]{2,1,0:T(8,128)S(1)}, u32[]{:S(2)}, u32[]{:S(2)}) collective-permute-start(f32[8,64,128]{2,1,0:T(8,128)S(1)} %shard_map.63), channel_id=1, source_target_pairs={{0,8},{8,0},{1,9},{9,1},{2,10},{10,2},{3,11},{11,3},{4,12},{12,4},... | collective-permute-start | bytes 786440 | tf_op jit(solution)/shard_map/ppermute | solution.py:204
  63.0 13.3 %collective-permute-start.17 = (f32[8,64,128]{2,1,0:T(8,128)S(1)}, f32[8,64,128]{2,1,0:T(8,128)S(1)}, u32[]{:S(2)}, u32[]{:S(2)}) collective-permute-start(f32[8,64,128]{2,1,0:T(8,128)S(1)} %collective-permute-done.12.refs_1_), channel_id=1, source_target_pairs={{0,8},{8,0},{1,9},{9,1},{2,10},{10,2},{3,11},{11,3},{4,12},{12,4},... | collective-permute-start | bytes 786440 | tf_op jit(solution)/shard_map/ppermute | solution.py:204
  63.6 18.4 %collective-permute-start.18 = (f32[8,64,128]{2,1,0:T(8,128)S(1)}, f32[8,64,128]{2,1,0:T(8,128)S(1)}, u32[]{:S(2)}, u32[]{:S(2)}) collective-permute-start(f32[8,64,128]{2,1,0:T(8,128)S(1)} %collective-permute-done.13.refs_2_), channel_id=1, source_target_pairs={{0,8},{8,0},{1,9},{9,1},{2,10},{10,2},{3,11},{11,3},{4,12},{12,4},... | collective-permute-start | bytes 786440 | tf_op jit(solution)/shard_map/ppermute | solution.py:204
  67.3 19.1 %collective-permute-start.19 = (f32[8,64,128]{2,1,0:T(8,128)S(1)}, f32[8,64,128]{2,1,0:T(8,128)S(1)}, u32[]{:S(2)}, u32[]{:S(2)}) collective-permute-start(f32[8,64,128]{2,1,0:T(8,128)S(1)} %broadcast_select_fusion.refs_0_), channel_id=1, source_target_pairs={{0,8},{8,0},{1,9},{9,1},{2,10},{10,2},{3,11},{11,3},{4,12},{12,4},... | collective-permute-start | bytes 786440 | tf_op jit(solution)/shard_map/ppermute | solution.py:204
  69.5 17.7 %collective-permute-start.20 = (f32[4,64,128]{2,1,0:T(8,128)S(1)}, f32[4,64,128]{2,1,0:T(8,128)S(1)}, u32[]{:S(2)}, u32[]{:S(2)}) collective-permute-start(f32[4,64,128]{2,1,0:T(8,128)S(1)} %get-tuple-element.44), channel_id=1, source_target_pairs={{0,1},{1,0},{2,3},{3,2},{4,5},{5,4},{6,7},{7,6},{8,9},{9,8},{10,11... | collective-permute-start | bytes 393224 | tf_op jit(solution)/shard_map/ppermute | solution.py:207
  87.2 1.4 %collective-permute-start.21 = (f32[4,64,128]{2,1,0:T(8,128)S(1)}, f32[4,64,128]{2,1,0:T(8,128)S(1)}, u32[]{:S(2)}, u32[]{:S(2)}) collective-permute-start(f32[4,64,128]{2,1,0:T(8,128)S(1)} %get-tuple-element.46), channel_id=1, source_target_pairs={{0,1},{1,0},{2,3},{3,2},{4,5},{5,4},{6,7},{7,6},{8,9},{9,8},{10,11... | collective-permute-start | bytes 393224 | tf_op jit(solution)/shard_map/ppermute | solution.py:207

commit v2 on v1

--- a/solution.py
+++ b/solution.py
@@ -41,15 +41,15 @@
     return high, (x - high.astype(jnp.float32)).astype(jnp.bfloat16)
 
 
-def products(piece_parts, slot, part_refs, blocks, size):
+def products(piece_parts, slot, part_refs, blocks, size, lower=0, upper=None):
     high, _, both = piece_parts
     front = high.shape[0]
     first = slot * blocks
     out = []
     high_ref, low_ref = part_refs
-    columns = high_ref.shape[2]
-    step = min(columns, 2 * size)
-    for at in range(0, columns, step):
+    upper = high_ref.shape[2] // size if upper is None else upper
+    step = (2 if (upper - lower) % 2 == 0 else 1) * size
+    for at in range(lower * size, upper * size, step):
         w_high = high_ref[first:first + blocks, :, at:at + step].reshape(blocks * size, step)
         w_low = low_ref[first:first + blocks, :, at:at + step].reshape(blocks * size, step)
         product = jnp.dot(both, w_high, preferred_element_type=jnp.float32)
@@ -63,8 +63,10 @@
     return high, low, jnp.concatenate([high, low], axis=0)
 
 
-def added(base, pieces, slots, parts):
-    blocks, _, size = base.shape
+def added(base, pieces, slots, parts, lower=0, upper=None, unless=None):
+    blocks, front, size = base.shape
+    upper = blocks if upper is None else upper
+    unless = () if unless is None else unless
 
     def kernel(base_ref, *refs):
         n = len(pieces)
@@ -72,18 +74,46 @@
         total = None
         for i in range(n):
             piece = piece_parts(jnp.concatenate([refs[i][p] for p in range(blocks)], axis=1))
-            terms = products(piece, slots[i], refs[n:n + 2], blocks, size)
+            terms = products(piece, slots[i], refs[n:n + 2], blocks, size, lower, upper)
             total = terms if total is None else [t + u for t, u in zip(total, terms)]
-        for i in range(blocks):
-            out_ref[i] = base_ref[i] + total[i]
-
-    return pl.pallas_call(
-        kernel,
-        out_shape=jax.ShapeDtypeStruct(base.shape, jnp.float32),
-        in_specs=[IN_VMEM] * (len(pieces) + 3),
+        for i in range(upper - lower):
+            value = base_ref[lower + i] + total[i]
+            out_ref[i] = jnp.where(refs[n + 2][0] != 0, refs[n + 3][lower + i], value) if unless else value
+
+    return pl.pallas_call(
+        kernel,
+        out_shape=jax.ShapeDtypeStruct((upper - lower, front, size), jnp.float32),
+        in_specs=[IN_VMEM] * (len(pieces) + 3) + [IN_SMEM, IN_VMEM][:len(unless)],
         out_specs=IN_VMEM,
         compiler_params=PARAMS,
-    )(base, *pieces, *parts)
+    )(base, *pieces, *parts, *unless)
+
+
+def stored(core_at, near, back, which, nreal, earlier=()):
+    blocks, quarter, size = near.shape
+    half = nreal // 2
+
+    def kernel(core_ref, near_ref, back_ref, *refs):
+        out_ref, sent = refs[-2:]
+        core = core_ref[0]
+        copies = []
+        for i, (ref, side) in enumerate(((near_ref, core), (back_ref, 1 - core))):
+            rows = pl.ds(pl.multiple_of(side * half + which * quarter, quarter), quarter)
+            copies.append(pltpu.make_async_copy(ref, out_ref.at[:, rows, :], sent.at[i]))
+        for copy in copies:
+            copy.start()
+        for copy in copies:
+            copy.wait()
+
+    return pl.pallas_call(
+        kernel,
+        out_shape=pltpu.HBM((blocks, nreal, size), jnp.float32),
+        in_specs=[IN_SMEM] + [IN_VMEM] * 2 + [IN_HBM] * len(earlier),
+        out_specs=IN_HBM,
+        scratch_shapes=[pltpu.SemaphoreType.DMA((2,))],
+        input_output_aliases={3: 0} if earlier else {},
+        compiler_params=PARAMS,
+    )(core_at, near, back, *earlier)
 
 
 def placed(turned_from, at, count, size, rows_ref, high_ref, low_ref):
@@ -216,9 +246,9 @@
         return ((there ^ place) * (2 * blocks) + (lax.div(inside, blocks) ^ core) * blocks + lax.rem(inside, blocks)).reshape(-1)
 
     rows = jnp.concatenate([rows_of(cond_lists), rows_of(lists_other)])
-    scalars = (slab == 0, (place == 0) | (place == 3), core == 0, core.reshape(1), core * half + slab * quarter, rows, mine)
+    scalars = (slab == 0, (slab == 0).astype(jnp.int32).reshape(1), (place == 0) | (place == 3), core.reshape(1), core * half + slab * quarter, rows, mine)
     scalars, start_other, regress, chol, noise = lax.optimization_barrier((scalars, start_other, regress, chol, noise))
-    on_first, at_end, core_first, core_at, first, rows, mine = scalars
+    on_first, first_at, at_end, core_at, first, rows, mine = scalars
     chol_other = partner(chol)
     noise_other = partner(noise)
     regress_other = partner(regress)
@@ -254,17 +284,13 @@
     direct_b = added(shock_1, [crossed, f1, f2], [0, 1, 3], parts)
     direct_b = added(direct_b, [f3], [2], parts)
     routed_b = added(shock_2, [own_x, f1_x, f2_x], [0, 1, 3], parts)
-    routed_b = added(routed_b, [f3_x], [2], parts)
-
-    def home(x):
-        back = partner(x[blocks:])
-        return x[:blocks], back
-
-    near_a, back_a = home(jnp.where(on_first, direct, direct_b))
-    near_b, back_b = home(jnp.where(on_first, routed, routed_b))
-    near = jnp.concatenate([near_a, near_b], 1)
-    back = jnp.concatenate([back_a, back_b], 1)
-    return jnp.where(core_first, jnp.concatenate([near, back], 1), jnp.concatenate([back, near], 1))
+    near_a = jnp.where(on_first, direct[:blocks], direct_b[:blocks])
+    back_a = partner(jnp.where(on_first, direct[blocks:], direct_b[blocks:]))
+    out = stored(core_at, near_a, back_a, 0, nreal)
+    far_b = added(routed_b, [f3_x], [2], parts, blocks, 2 * blocks, (first_at, routed))
+    back_b = partner(far_b)
+    near_b = added(routed_b, [f3_x], [2], parts, 0, blocks, (first_at, routed))
+    return stored(core_at, near_b, back_b, 1, nreal, (out,))
 
 
 def solution(mesh):

time: 89.7 us -> 89.9 us (level)
  starting transfers between devices: 29.8 us -> 23.6 us
  waiting for transfers between devices: 36.5 us -> 42.1 us
  Pallas kernels: 19.9 us -> 21.5 us
    ppermute x8, waiting for transfers between devices: 15.1 us -> 23.4 us  [along_lat(): return lambda x: lax.ppermute(x, 'lat', wires)]
    ppermute x8, starting transfers between devices: 20.2 us -> 14.1 us  [along_lat(): return lambda x: lax.ppermute(x, 'lat', wires)]
    pallas_call x8 -> x11, Pallas kernels: 10.4 us -> 12 us  [the longest x9 10.5 us: added(): pl.pallas_call(kernel, out_shape=jax.ShapeDtypeStruct((upper - lower, fro...]
    ppermute x7, waiting for transfers between devices: 19.8 us -> 18.4 us  [across(): return lax.ppermute(x, 'slab', [(0, 1), (1, 0)])]
    ppermute x7, waiting for transfers between devices: 1.55 us -> 0.35 us  [partner(): return lax.ppermute(x, 'lat', [(i, i ^ 1) for i in range(8)])]
  transfers between devices with their start and end apart: 22 -> 22, of which waited for: 12 -> 14; matrix products, arithmetic and copies ran while one was open for 2% -> 2% of each run, Pallas kernels for 21% -> 22%
where the time goes in v2:
time: 89.9 us; the launch traced here: 89.7 us
  waiting for transfers between devices  42.1 us (47%)
  starting transfers between devices  23.6 us (26%)
  Pallas kernels  21.5 us (24%)
  local copies, waits for them, and re-layouts  1.1 us (1%)
  other arithmetic  0.97 us (1%)
    ppermute x8, waiting for transfers between devices, along_lat(): return lambda x: lax.ppermute(x, 'lat', wires)  23.4 us
    ppermute x7, waiting for transfers between devices, across(): return lax.ppermute(x, 'slab', [(0, 1), (1, 0)])  18.4 us
    ppermute x8, starting transfers between devices, along_lat(): return lambda x: lax.ppermute(x, 'lat', wires)  14.1 us
    pallas_call x9, Pallas kernels, added(): pl.pallas_call(kernel, out_shape=jax.ShapeDtypeStruct((upper - lower, fro...  10.5 us
    ppermute x7, starting transfers between devices, across(): return lax.ppermute(x, 'slab', [(0, 1), (1, 0)])  8.61 us
    pallas_call x1, Pallas kernels, weights_other(): pl.pallas_call(kernel, out_shape=(part,) * 2, in_specs=[IN_SMEM] + [IN_VM...  3.69 us
    pallas_call x1, Pallas kernels, weights(): pl.pallas_call(kernel, out_shape=(part,) * 2, in_specs=[IN_SMEM, IN_HBM],...  3.53 us
    pallas_call x1, Pallas kernels, opening(): pl.pallas_call(kernel, out_shape=(piece,) * 4, in_specs=[IN_SMEM] + [IN_V...  2.33 us
  transfers between devices with their start and end apart: 22, of which 14 were waited for; matrix products, arithmetic and copies ran while one was open for 2% of the time, Pallas kernels for 22%

profile of v2, /device:TPU:0, one launch (start us, length us, event | category | flops | bytes accessed | tf_op | source)
XLA Modules:
  0.0 89.7 jit_solution(3711907527001783467)
XLA Ops:
  0.5 0.9 %constant_dynamic-slice_fusion.1 = f32[4,64,128]{2,1,0:T(8,128)S(1)} fusion(f32[4,256,128]{2,1,0:T(8,128)} %start_hbm.1, s32[]{:T(128)S(6)} %select_n.40), kind=kLoop, calls=%fused_computation.33 | loop fusion | bytes 262148 | tf_op jit(solution)/shard_map/dynamic_slice | solution.py:240
  2.9 2.8 %collective-permute-start.5 = (f32[8,64,128]{2,1,0:T(8,128)S(1)}, f32[8,64,128]{2,1,0:T(8,128)S(1)}, u32[]{:S(2)}, u32[]{:S(2)}) collective-permute-start(f32[8,64,128]{2,1,0:T(8,128)S(1)} %pad_maximum_fusion), channel_id=1, source_target_pairs={{0,2},{1,3},{4,6},{5,7},{2,0},{3,1},{6,4},{7,5},{8,10},{9,11},{12,... | collective-permute-start | bytes 786440 | tf_op jit(solution)/shard_map/ppermute | solution.py:229
  5.8 2.5 %collective-permute-start.7 = (f32[8,64,128]{2,1,0:T(8,128)S(1)}, f32[8,64,128]{2,1,0:T(8,128)S(1)}, u32[]{:S(2)}, u32[]{:S(2)}) collective-permute-start(f32[8,64,128]{2,1,0:T(8,128)S(1)} %pad_maximum_fusion), channel_id=1, source_target_pairs={{0,6},{1,7},{2,4},{3,5},{6,0},{7,1},{4,2},{5,3},{8,14},{9,15},{10,... | collective-permute-start | bytes 786440 | tf_op jit(solution)/shard_map/ppermute | solution.py:229
  8.3 4.3 %collective-permute-done.5.refs_0_ = f32[8,64,128]{2,1,0:T(8,128)S(1)} collective-permute-done((f32[8,64,128]{2,1,0:T(8,128)S(1)}, f32[8,64,128]{2,1,0:T(8,128)S(1)}, u32[]{:S(2)}, u32[]{:S(2)}) %collective-permute-start.5) | collective-permute-done | bytes 262176 | tf_op jit(solution)/shard_map/ppermute | solution.py:229
  13.2 7.2 %collective-permute-done.7.refs_1_ = f32[8,64,128]{2,1,0:T(8,128)S(1)} collective-permute-done((f32[8,64,128]{2,1,0:T(8,128)S(1)}, f32[8,64,128]{2,1,0:T(8,128)S(1)}, u32[]{:S(2)}, u32[]{:S(2)}) %collective-permute-start.7) | collective-permute-done | bytes 262176 | tf_op jit(solution)/shard_map/ppermute | solution.py:229
  20.5 0.8 collective-permute-start.9
  21.3 3.5 %weights.1 = (bf16[32,128,1024]{2,1,0:T(8,128)(2,1)S(1)}, bf16[32,128,1024]{2,1,0:T(8,128)(2,1)S(1)}) custom-call(s32[128]{0:T(128)S(1)} %pad_add_fusion.rows_ref, f32[4,128,2048]{2,1,0:T(8,128)} %regress_ref), custom_call_target="tpu_custom_call" | custom-call | tf_op jit(solution)/shard_map/weights/pallas_call | solution.py:145
  24.8 1.6 %collective-permute-start.6 = (f32[8,64,128]{2,1,0:T(8,128)S(1)}, f32[8,64,128]{2,1,0:T(8,128)S(1)}, u32[]{:S(2)}, u32[]{:S(2)}) collective-permute-start(f32[8,64,128]{2,1,0:T(8,128)S(1)} %collective-permute-done.5.refs_0_), channel_id=1, source_target_pairs={{0,8},{8,0},{1,9},{9,1},{2,10},{10,2},{3,11},{11,3},{4,12},{12,4},... | collective-permute-start | bytes 786440 | tf_op jit(solution)/shard_map/ppermute | solution.py:234
  26.4 1.7 %collective-permute-done.9 = f32[8,64,128]{2,1,0:T(8,128)S(1)} collective-permute-done((f32[8,64,128]{2,1,0:T(8,128)S(1)}, f32[8,64,128]{2,1,0:T(8,128)S(1)}, u32[]{:S(2)}, u32[]{:S(2)}) %collective-permute-start.9) | collective-permute-done | bytes 262176 | tf_op jit(solution)/shard_map/ppermute | solution.py:229
  28.0 1.5 %collective-permute-start.8 = (f32[8,64,128]{2,1,0:T(8,128)S(1)}, f32[8,64,128]{2,1,0:T(8,128)S(1)}, u32[]{:S(2)}, u32[]{:S(2)}) collective-permute-start(f32[8,64,128]{2,1,0:T(8,128)S(1)} %collective-permute-done.7.refs_1_), channel_id=1, source_target_pairs={{0,8},{8,0},{1,9},{9,1},{2,10},{10,2},{3,11},{11,3},{4,12},{12,4},... | collective-permute-start | bytes 786440 | tf_op jit(solution)/shard_map/ppermute | solution.py:234
  29.6 3.7 %weights_other.1 = (bf16[32,128,1024]{2,1,0:T(8,128)(2,1)S(1)}, bf16[32,128,1024]{2,1,0:T(8,128)(2,1)S(1)}) custom-call(s32[128]{0:T(128)S(1)} %pad_add_fusion.rows_ref, bf16[32,128,1024]{2,1,0:T(8,128)(2,1)S(1)} %get-tuple-element.27.high_in, bf16[32,128,1024]{2,1,0:T(8,128)(2,1)S(1)} %get-tuple-element.28.low_in, ...), custom_call_target="tpu_custom_call", output_to_operand_aliasing={{0}: (1, {}), {1}: (2, {})} | custom-call | tf_op jit(solution)/shard_map/weights_other/pallas_call | solution.py:166
  33.3 2.3 %opening.1 = (f32[8,64,128]{2,1,0:T(8,128)S(1)}, f32[8,64,128]{2,1,0:T(8,128)S(1)}, f32[8,64,128]{2,1,0:T(8,128)S(1)}, f32[8,64,128]{2,1,0:T(8,128)S(1)}) custom-call(s32[1]{0:T(128)} %bitcast.1.core_ref, bf16[32,128,1024]{2,1,0:T(8,128)(2,1)S(1)} %get-tuple-element.29.high_ref.refs_2_.refs_1_.refs_3_, ...), custom_call_target="tpu_custom_call" | custom-call | tf_op jit(solution)/shard_map/opening/pallas_call | solution.py:208
  35.6 1.5 %shard_map.61.base_ref = f32[8,64,128]{2,1,0:T(8,128)S(1)} custom-call(f32[8,64,128]{2,1,0:T(8,128)S(1)} %get-tuple-element.39.base_ref, f32[8,64,128]{2,1,0:T(8,128)S(1)} %collective-permute-done.5.refs_0_, f32[8,64,128]{2,1,0:T(8,128)S(1)} %collective-permute-done.7.refs_1_, bf16[32,128,1024]{2,1,0:T(8,128)(2,1)S(1)} %get-tuple-element.29.high_ref.refs_2_.refs_1_.refs_3_, ...), custom_call_target="tpu_custom_call" | custom-call | tf_op jit(solution)/shard_map/pallas_call | solution.py:83
  37.1 0.8 shard_map.62
  38.6 1.0 %collective-permute-done.8.refs_1_ = f32[8,64,128]{2,1,0:T(8,128)S(1)} collective-permute-done((f32[8,64,128]{2,1,0:T(8,128)S(1)}, f32[8,64,128]{2,1,0:T(8,128)S(1)}, u32[]{:S(2)}, u32[]{:S(2)}) %collective-permute-start.8) | collective-permute-done | bytes 262176 | tf_op jit(solution)/shard_map/ppermute | solution.py:234
  39.6 1.5 %shard_map.60.base_ref = f32[8,64,128]{2,1,0:T(8,128)S(1)} custom-call(f32[8,64,128]{2,1,0:T(8,128)S(1)} %get-tuple-element.35.base_ref, f32[8,64,128]{2,1,0:T(8,128)S(1)} %collective-permute-done.6.refs_0_, f32[8,64,128]{2,1,0:T(8,128)S(1)} %collective-permute-done.8.refs_1_, bf16[32,128,1024]{2,1,0:T(8,128)(2,1)S(1)} %get-tuple-element.29.high_ref.refs_2_.refs_1_.refs_3_, ...), custom_call_target="tpu_custom_call" | custom-call | tf_op jit(solution)/shard_map/pallas_call | solution.py:83
  41.1 3.8 %collective-permute-done.11.refs_0_ = f32[8,64,128]{2,1,0:T(8,128)S(1)} collective-permute-done((f32[8,64,128]{2,1,0:T(8,128)S(1)}, f32[8,64,128]{2,1,0:T(8,128)S(1)}, u32[]{:S(2)}, u32[]{:S(2)}) %collective-permute-start.11) | collective-permute-done | bytes 262176 | tf_op jit(solution)/shard_map/ppermute | solution.py:234
  45.7 3.4 %collective-permute-start.15 = (f32[8,64,128]{2,1,0:T(8,128)S(1)}, f32[8,64,128]{2,1,0:T(8,128)S(1)}, u32[]{:S(2)}, u32[]{:S(2)}) collective-permute-start(f32[8,64,128]{2,1,0:T(8,128)S(1)} %broadcast_select_fusion.2), channel_id=1, source_target_pairs={{0,6},{1,7},{2,4},{3,5},{6,0},{7,1},{4,2},{5,3},{8,14},{9,15},{10,... | collective-permute-start | bytes 786440 | tf_op jit(solution)/shard_map/ppermute | solution.py:229
  49.1 7.6 %collective-permute-done.15.refs_2_ = f32[8,64,128]{2,1,0:T(8,128)S(1)} collective-permute-done((f32[8,64,128]{2,1,0:T(8,128)S(1)}, f32[8,64,128]{2,1,0:T(8,128)S(1)}, u32[]{:S(2)}, u32[]{:S(2)}) %collective-permute-start.15) | collective-permute-done | bytes 262176 | tf_op jit(solution)/shard_map/ppermute | solution.py:229
  56.8 3.0 %collective-permute-start.17 = (f32[8,64,128]{2,1,0:T(8,128)S(1)}, f32[8,64,128]{2,1,0:T(8,128)S(1)}, u32[]{:S(2)}, u32[]{:S(2)}) collective-permute-start(f32[8,64,128]{2,1,0:T(8,128)S(1)} %collective-permute-done.15.refs_2_), channel_id=1, source_target_pairs={{0,2},{1,3},{4,6},{5,7},{2,0},{3,1},{6,4},{7,5},{8,10},{9,11},{12,... | collective-permute-start | bytes 786440 | tf_op jit(solution)/shard_map/ppermute | solution.py:229
  59.8 1.7 %collective-permute-done.13.refs_1_ = f32[8,64,128]{2,1,0:T(8,128)S(1)} collective-permute-done((f32[8,64,128]{2,1,0:T(8,128)S(1)}, f32[8,64,128]{2,1,0:T(8,128)S(1)}, u32[]{:S(2)}, u32[]{:S(2)}) %collective-permute-start.13) | collective-permute-done | bytes 262176 | tf_op jit(solution)/shard_map/ppermute | solution.py:229
  61.4 0.8 collective-permute-start.18
  62.3 1.4 %collective-permute-start.12 = (f32[8,64,128]{2,1,0:T(8,128)S(1)}, f32[8,64,128]{2,1,0:T(8,128)S(1)}, u32[]{:S(2)}, u32[]{:S(2)}) collective-permute-start(f32[8,64,128]{2,1,0:T(8,128)S(1)} %shard_map.63.refs_4_), channel_id=1, source_target_pairs={{0,8},{8,0},{1,9},{9,1},{2,10},{10,2},{3,11},{11,3},{4,12},{12,4},... | collective-permute-start | bytes 786440 | tf_op jit(solution)/shard_map/ppermute | solution.py:234
  64.4 1.3 %collective-permute-start.16 = (f32[8,64,128]{2,1,0:T(8,128)S(1)}, f32[8,64,128]{2,1,0:T(8,128)S(1)}, u32[]{:S(2)}, u32[]{:S(2)}) collective-permute-start(f32[8,64,128]{2,1,0:T(8,128)S(1)} %collective-permute-done.15.refs_2_), channel_id=1, source_target_pairs={{0,8},{8,0},{1,9},{9,1},{2,10},{10,2},{3,11},{11,3},{4,12},{12,4},... | collective-permute-start | bytes 786440 | tf_op jit(solution)/shard_map/ppermute | solution.py:234
  65.7 0.9 collective-permute-done.17
  66.6 1.6 %collective-permute-start.19 = (f32[8,64,128]{2,1,0:T(8,128)S(1)}, f32[8,64,128]{2,1,0:T(8,128)S(1)}, u32[]{:S(2)}, u32[]{:S(2)}) collective-permute-start(f32[8,64,128]{2,1,0:T(8,128)S(1)} %broadcast_select_fusion.refs_0_), channel_id=1, source_target_pairs={{0,8},{8,0},{1,9},{9,1},{2,10},{10,2},{3,11},{11,3},{4,12},{12,4},... | collective-permute-start | bytes 786440 | tf_op jit(solution)/shard_map/ppermute | solution.py:234
  68.2 2.2 %shard_map.67.base_ref = f32[8,64,128]{2,1,0:T(8,128)S(1)} custom-call(f32[8,64,128]{2,1,0:T(8,128)S(1)} %get-tuple-element.42.base_ref, f32[8,64,128]{2,1,0:T(8,128)S(1)} %collective-permute-done.11.refs_0_, f32[8,64,128]{2,1,0:T(8,128)S(1)} %collective-permute-done.13.refs_1_, f32[8,64,128]{2,1,0:T(8,128)S(1)} %collective-permute-done.15.refs_2_, ...), custom_call_target="tpu_custom_call" | custom-call | tf_op jit(solution)/shard_map/pallas_call | solution.py:83
  70.3 0.8 shard_map.68
  71.5 5.6 %collective-permute-done.14.refs_1_ = f32[8,64,128]{2,1,0:T(8,128)S(1)} collective-permute-done((f32[8,64,128]{2,1,0:T(8,128)S(1)}, f32[8,64,128]{2,1,0:T(8,128)S(1)}, u32[]{:S(2)}, u32[]{:S(2)}) %collective-permute-start.14) | collective-permute-done | bytes 262176 | tf_op jit(solution)/shard_map/ppermute | solution.py:234
  77.1 5.6 %collective-permute-done.16.refs_2_ = f32[8,64,128]{2,1,0:T(8,128)S(1)} collective-permute-done((f32[8,64,128]{2,1,0:T(8,128)S(1)}, f32[8,64,128]{2,1,0:T(8,128)S(1)}, u32[]{:S(2)}, u32[]{:S(2)}) %collective-permute-start.16) | collective-permute-done | bytes 262176 | tf_op jit(solution)/shard_map/ppermute | solution.py:234
  82.8 2.1 %shard_map.64.base_ref = f32[8,64,128]{2,1,0:T(8,128)S(1)} custom-call(f32[8,64,128]{2,1,0:T(8,128)S(1)} %get-tuple-element.34.base_ref, f32[8,64,128]{2,1,0:T(8,128)S(1)} %collective-permute-done.12.refs_0_, f32[8,64,128]{2,1,0:T(8,128)S(1)} %collective-permute-done.14.refs_1_, f32[8,64,128]{2,1,0:T(8,128)S(1)} %collective-permute-done.16.refs_2_, ...), custom_call_target="tpu_custom_call" | custom-call | tf_op jit(solution)/shard_map/pallas_call | solution.py:83
  84.9 2.0 %collective-permute-done.19.refs_0_ = f32[8,64,128]{2,1,0:T(8,128)S(1)} collective-permute-done((f32[8,64,128]{2,1,0:T(8,128)S(1)}, f32[8,64,128]{2,1,0:T(8,128)S(1)}, u32[]{:S(2)}, u32[]{:S(2)}) %collective-permute-start.19) | collective-permute-done | bytes 262176 | tf_op jit(solution)/shard_map/ppermute | solution.py:234
  (39 shorter events, 7.8 us)
Async XLA Ops:
  0.0 2.2 %collective-permute-start = (s32[4,16]{1,0:T(4,128)}, s32[4,16]{1,0:T(4,128)S(1)}, u32[]{:S(2)}, u32[]{:S(2)}) collective-permute-start(s32[4,16]{1,0:T(4,128)} %param.5), channel_id=1, source_target_pairs={{0,1},{1,0},{2,3},{3,2},{4,5},{5,4},{6,7},{7,6},{8,9},{9,8},{10,11... | collective-permute-start | bytes 776 | tf_op jit(solution)/shard_map/ppermute | solution.py:237
  0.5 2.1 %collective-permute-start.1 = (f32[4,256,128]{2,1,0:T(8,128)}, f32[4,256,128]{2,1,0:T(8,128)S(1)}, u32[]{:S(2)}, u32[]{:S(2)}) collective-permute-start(f32[4,256,128]{2,1,0:T(8,128)} %start_hbm.1), channel_id=1, source_target_pairs={{0,1},{1,0},{2,3},{3,2},{4,5},{5,4},{6,7},{7,6},{8,9},{9,8},{10,11... | collective-permute-start | bytes 1572872 | tf_op jit(solution)/shard_map/ppermute | solution.py:237
  2.6 27.0 %collective-permute-start.2 = (f32[4,128,2048]{2,1,0:T(8,128)}, f32[4,128,2048]{2,1,0:T(8,128)}, u32[]{:S(2)}, u32[]{:S(2)}) collective-permute-start(f32[4,128,2048]{2,1,0:T(8,128)} %regress_ref), channel_id=1, source_target_pairs={{0,1},{1,0},{2,3},{3,2},{4,5},{5,4},{6,7},{7,6},{8,9},{9,8},{10,11... | collective-permute-start | bytes 12582920 | tf_op jit(solution)/shard_map/ppermute | solution.py:237
  2.9 9.6 %collective-permute-start.5 = (f32[8,64,128]{2,1,0:T(8,128)S(1)}, f32[8,64,128]{2,1,0:T(8,128)S(1)}, u32[]{:S(2)}, u32[]{:S(2)}) collective-permute-start(f32[8,64,128]{2,1,0:T(8,128)S(1)} %pad_maximum_fusion), channel_id=1, source_target_pairs={{0,2},{1,3},{4,6},{5,7},{2,0},{3,1},{6,4},{7,5},{8,10},{9,11},{12,... | collective-permute-start | bytes 786440 | tf_op jit(solution)/shard_map/ppermute | solution.py:229
  5.8 14.7 %collective-permute-start.7 = (f32[8,64,128]{2,1,0:T(8,128)S(1)}, f32[8,64,128]{2,1,0:T(8,128)S(1)}, u32[]{:S(2)}, u32[]{:S(2)}) collective-permute-start(f32[8,64,128]{2,1,0:T(8,128)S(1)} %pad_maximum_fusion), channel_id=1, source_target_pairs={{0,6},{1,7},{2,4},{3,5},{6,0},{7,1},{4,2},{5,3},{8,14},{9,15},{10,... | collective-permute-start | bytes 786440 | tf_op jit(solution)/shard_map/ppermute | solution.py:229
  8.3 25.0 %collective-permute-start.4 = (f32[4,256,128]{2,1,0:T(8,128)}, f32[4,256,128]{2,1,0:T(8,128)S(1)}, u32[]{:S(2)}, u32[]{:S(2)}) collective-permute-start(f32[4,256,128]{2,1,0:T(8,128)} %noise_hbm), channel_id=1, source_target_pairs={{0,1},{1,0},{2,3},{3,2},{4,5},{5,4},{6,7},{7,6},{8,9},{9,8},{10,11... | collective-permute-start | bytes 1572872 | tf_op jit(solution)/shard_map/ppermute | solution.py:237
  12.6 12.3 %collective-permute-start.10 = (f32[8,64,128]{2,1,0:T(8,128)S(1)}, f32[8,64,128]{2,1,0:T(8,128)S(1)}, u32[]{:S(2)}, u32[]{:S(2)}) collective-permute-start(f32[8,64,128]{2,1,0:T(8,128)S(1)} %collective-permute-done.5.refs_0_), channel_id=1, source_target_pairs={{2,4},{3,5},{4,2},{5,3},{10,12},{11,13},{12,10},{13,11},{18,20},{1... | collective-permute-start | bytes 786440 | tf_op jit(solution)/shard_map/ppermute | solution.py:229
  20.5 7.6 %collective-permute-start.9 = (f32[8,64,128]{2,1,0:T(8,128)S(1)}, f32[8,64,128]{2,1,0:T(8,128)S(1)}, u32[]{:S(2)}, u32[]{:S(2)}) collective-permute-start(f32[8,64,128]{2,1,0:T(8,128)S(1)} %collective-permute-done.7.refs_1_), channel_id=1, source_target_pairs={{0,2},{1,3},{4,6},{5,7},{2,0},{3,1},{6,4},{7,5},{8,10},{9,11},{12,... | collective-permute-start | bytes 786440 | tf_op jit(solution)/shard_map/ppermute | solution.py:229
  21.3 12.0 %collective-permute-start.3 = (f32[4,128,128]{2,1,0:T(8,128)}, f32[4,128,128]{2,1,0:T(8,128)S(1)}, u32[]{:S(2)}, u32[]{:S(2)}) collective-permute-start(f32[4,128,128]{2,1,0:T(8,128)} %chol_hbm), channel_id=1, source_target_pairs={{0,1},{1,0},{2,3},{3,2},{4,5},{5,4},{6,7},{7,6},{8,9},{9,8},{10,11... | collective-permute-start | bytes 786440 | tf_op jit(solution)/shard_map/ppermute | solution.py:237
  24.8 13.7 %collective-permute-start.6 = (f32[8,64,128]{2,1,0:T(8,128)S(1)}, f32[8,64,128]{2,1,0:T(8,128)S(1)}, u32[]{:S(2)}, u32[]{:S(2)}) collective-permute-start(f32[8,64,128]{2,1,0:T(8,128)S(1)} %collective-permute-done.5.refs_0_), channel_id=1, source_target_pairs={{0,8},{8,0},{1,9},{9,1},{2,10},{10,2},{3,11},{11,3},{4,12},{12,4},... | collective-permute-start | bytes 786440 | tf_op jit(solution)/shard_map/ppermute | solution.py:234
  28.0 11.5 %collective-permute-start.8 = (f32[8,64,128]{2,1,0:T(8,128)S(1)}, f32[8,64,128]{2,1,0:T(8,128)S(1)}, u32[]{:S(2)}, u32[]{:S(2)}) collective-permute-start(f32[8,64,128]{2,1,0:T(8,128)S(1)} %collective-permute-done.7.refs_1_), channel_id=1, source_target_pairs={{0,8},{8,0},{1,9},{9,1},{2,10},{10,2},{3,11},{11,3},{4,12},{12,4},... | collective-permute-start | bytes 786440 | tf_op jit(solution)/shard_map/ppermute | solution.py:234
  38.0 6.9 %collective-permute-start.11 = (f32[8,64,128]{2,1,0:T(8,128)S(1)}, f32[8,64,128]{2,1,0:T(8,128)S(1)}, u32[]{:S(2)}, u32[]{:S(2)}) collective-permute-start(f32[8,64,128]{2,1,0:T(8,128)S(1)} %broadcast_select_fusion.3), channel_id=1, source_target_pairs={{0,8},{8,0},{1,9},{9,1},{2,10},{10,2},{3,11},{11,3},{4,12},{12,4},... | collective-permute-start | bytes 786440 | tf_op jit(solution)/shard_map/ppermute | solution.py:234
  45.7 11.1 %collective-permute-start.15 = (f32[8,64,128]{2,1,0:T(8,128)S(1)}, f32[8,64,128]{2,1,0:T(8,128)S(1)}, u32[]{:S(2)}, u32[]{:S(2)}) collective-permute-start(f32[8,64,128]{2,1,0:T(8,128)S(1)} %broadcast_select_fusion.2), channel_id=1, source_target_pairs={{0,6},{1,7},{2,4},{3,5},{6,0},{7,1},{4,2},{5,3},{8,14},{9,15},{10,... | collective-permute-start | bytes 786440 | tf_op jit(solution)/shard_map/ppermute | solution.py:229
  49.1 12.3 %collective-permute-start.13 = (f32[8,64,128]{2,1,0:T(8,128)S(1)}, f32[8,64,128]{2,1,0:T(8,128)S(1)}, u32[]{:S(2)}, u32[]{:S(2)}) collective-permute-start(f32[8,64,128]{2,1,0:T(8,128)S(1)} %broadcast_select_fusion.2), channel_id=1, source_target_pairs={{0,2},{1,3},{4,6},{5,7},{2,0},{3,1},{6,4},{7,5},{8,10},{9,11},{12,... | collective-permute-start | bytes 786440 | tf_op jit(solution)/shard_map/ppermute | solution.py:229
  56.8 9.8 %collective-permute-start.17 = (f32[8,64,128]{2,1,0:T(8,128)S(1)}, f32[8,64,128]{2,1,0:T(8,128)S(1)}, u32[]{:S(2)}, u32[]{:S(2)}) collective-permute-start(f32[8,64,128]{2,1,0:T(8,128)S(1)} %collective-permute-done.15.refs_2_), channel_id=1, source_target_pairs={{0,2},{1,3},{4,6},{5,7},{2,0},{3,1},{6,4},{7,5},{8,10},{9,11},{12,... | collective-permute-start | bytes 786440 | tf_op jit(solution)/shard_map/ppermute | solution.py:229
  61.4 5.2 %collective-permute-start.18 = (f32[8,64,128]{2,1,0:T(8,128)S(1)}, f32[8,64,128]{2,1,0:T(8,128)S(1)}, u32[]{:S(2)}, u32[]{:S(2)}) collective-permute-start(f32[8,64,128]{2,1,0:T(8,128)S(1)} %collective-permute-done.13.refs_1_), channel_id=1, source_target_pairs={{2,4},{3,5},{4,2},{5,3},{10,12},{11,13},{12,10},{13,11},{18,20},{1... | collective-permute-start | bytes 786440 | tf_op jit(solution)/shard_map/ppermute | solution.py:229
  62.3 9.2 %collective-permute-start.12 = (f32[8,64,128]{2,1,0:T(8,128)S(1)}, f32[8,64,128]{2,1,0:T(8,128)S(1)}, u32[]{:S(2)}, u32[]{:S(2)}) collective-permute-start(f32[8,64,128]{2,1,0:T(8,128)S(1)} %shard_map.63.refs_4_), channel_id=1, source_target_pairs={{0,8},{8,0},{1,9},{9,1},{2,10},{10,2},{3,11},{11,3},{4,12},{12,4},... | collective-permute-start | bytes 786440 | tf_op jit(solution)/shard_map/ppermute | solution.py:234
  63.7 13.5 %collective-permute-start.14 = (f32[8,64,128]{2,1,0:T(8,128)S(1)}, f32[8,64,128]{2,1,0:T(8,128)S(1)}, u32[]{:S(2)}, u32[]{:S(2)}) collective-permute-start(f32[8,64,128]{2,1,0:T(8,128)S(1)} %collective-permute-done.13.refs_1_), channel_id=1, source_target_pairs={{0,8},{8,0},{1,9},{9,1},{2,10},{10,2},{3,11},{11,3},{4,12},{12,4},... | collective-permute-start | bytes 786440 | tf_op jit(solution)/shard_map/ppermute | solution.py:234
  64.4 18.4 %collective-permute-start.16 = (f32[8,64,128]{2,1,0:T(8,128)S(1)}, f32[8,64,128]{2,1,0:T(8,128)S(1)}, u32[]{:S(2)}, u32[]{:S(2)}) collective-permute-start(f32[8,64,128]{2,1,0:T(8,128)S(1)} %collective-permute-done.15.refs_2_), channel_id=1, source_target_pairs={{0,8},{8,0},{1,9},{9,1},{2,10},{10,2},{3,11},{11,3},{4,12},{12,4},... | collective-permute-start | bytes 786440 | tf_op jit(solution)/shard_map/ppermute | solution.py:234
  66.6 20.3 %collective-permute-start.19 = (f32[8,64,128]{2,1,0:T(8,128)S(1)}, f32[8,64,128]{2,1,0:T(8,128)S(1)}, u32[]{:S(2)}, u32[]{:S(2)}) collective-permute-start(f32[8,64,128]{2,1,0:T(8,128)S(1)} %broadcast_select_fusion.refs_0_), channel_id=1, source_target_pairs={{0,8},{8,0},{1,9},{9,1},{2,10},{10,2},{3,11},{11,3},{4,12},{12,4},... | collective-permute-start | bytes 786440 | tf_op jit(solution)/shard_map/ppermute | solution.py:234
  71.2 16.3 %collective-permute-start.21 = (f32[4,64,128]{2,1,0:T(8,128)S(1)}, f32[4,64,128]{2,1,0:T(8,128)S(1)}, u32[]{:S(2)}, u32[]{:S(2)}) collective-permute-start(f32[4,64,128]{2,1,0:T(8,128)S(1)} %get-tuple-element.43), channel_id=1, source_target_pairs={{0,1},{1,0},{2,3},{3,2},{4,5},{5,4},{6,7},{7,6},{8,9},{9,8},{10,11... | collective-permute-start | bytes 393224 | tf_op jit(solution)/shard_map/ppermute | solution.py:237
  87.4 1.4 %collective-permute-start.20 = (f32[4,64,128]{2,1,0:T(8,128)S(1)}, f32[4,64,128]{2,1,0:T(8,128)S(1)}, u32[]{:S(2)}, u32[]{:S(2)}) collective-permute-start(f32[4,64,128]{2,1,0:T(8,128)S(1)} %shard_map.66), channel_id=1, source_target_pairs={{0,1},{1,0},{2,3},{3,2},{4,5},{5,4},{6,7},{7,6},{8,9},{9,8},{10,11... | collective-permute-start | bytes 393224 | tf_op jit(solution)/shard_map/ppermute | solution.py:237
